TPU v7x, 32 devices: a whole 2x2x4 slice. The times are simulated.
32 devices in a mesh: island: 8 (over z, x), mp: 4 (over y, core).
Axes of the slice: x: 2, y: 2, z: 4, core: 2. Of those that a mesh axis runs over, the one named last changes fastest.
Arguments:
- acts: bfloat16 [8, 1024, 8192], P('island', None, 'mp'), may hold values from -6 to 6
- queries: bfloat16 [8, 1024, 4096], P('island', None, 'mp'), may hold values from -41 to 41
- keys_values: bfloat16 [8, 1024, 1024], P('island', 'mp'), may hold values from -4 to 4
- out_grad: bfloat16 [8, 1024, 4096], P('island', None, 'mp'), may hold values from -6 to 6
- segments: int32 [8, 1024], P('island'), may hold values from 0 to 15, never falling along the last dimension, each value on 1 to 512 neighbouring positions
- drift: bfloat16 [8, 8192, 1024], P('island', 'mp'), may hold values from -1.1953125 to 1.1953125
- outer_weights: float32 [4, 2048, 1024], P('mp', 'island'), may hold values from -6 to 6
- momentum: float32 [4, 2048, 1024], P('mp', 'island'), may hold values from -1.2 to 1.2
Outputs:
- query_grads: bfloat16 [8, 1024, 4096], P('island', None, 'mp')
- new_outer: float32 [4, 2048, 1024], P('mp', 'island')
- new_momentum: float32 [4, 2048, 1024], P('mp', 'island')
- next_weights: bfloat16 [4, 2048, 1024], P('mp')
Inputs may be any that keep to these rules, and one draw needn't show every extreme that they name: `segments`: document ids never fall along a sequence.
All inputs are finite; a program needn't handle non-finite values.
Results may differ from a plain program's by a relative error of at most 0.0085.
Values may be sent and summed in bfloat16 or wider, within the bound.
No kernel may reach another device: no remote copies, remote signals or barrier semaphores. Data moves between devices by JAX's collectives and lax.ppermute only.
A program may use at most 192 MiB of HBM per device.

v0:
```python
import math

import jax
import jax.numpy as jnp
from jax import lax
from jax.sharding import PartitionSpec as P

D = 8192
HD = 128
QH = 32
KVH = 4


INNER_LR = 0.8
OUTER_LR = 0.7
MOMENTUM = 0.9
ROPE_BASE = 500000.0


def rope_tables(positions, head_width):
    half_width = head_width // 2
    exponent = jnp.arange(half_width, dtype=jnp.float32) * (2.0 / head_width)
    frequency = jnp.power(jnp.float32(ROPE_BASE), -exponent)
    angles = jnp.arange(positions, dtype=jnp.float32)[:, None] * frequency[None, :]
    return (jnp.cos(angles), jnp.sin(angles))


def unrotate(grads, cosine, sine_table):
    half_width = grads.shape[-1] // 2
    first_half = grads[..., :half_width]
    second_half = grads[..., half_width:]
    cos_wide = cosine[:, None, :]
    sin_wide = sine_table[:, None, :]
    return jnp.concatenate(
        [
            first_half * cos_wide + second_half * sin_wide,
            second_half * cos_wide - first_half * sin_wide,
        ],
        axis=-1,
    )


def attention_probs(query_rows, key_cols, segment_ids, score_scale):
    positions = jnp.arange(segment_ids.shape[0])
    allowed = (positions[:, None] >= positions[None, :]) & (
        segment_ids[:, None] == segment_ids[None, :]
    )
    scores = (
        jnp.einsum("qhd,kd->hqk", query_rows, key_cols, preferred_element_type=jnp.float32)
        * score_scale
    )
    scores = jnp.where(allowed[None], scores, -jnp.inf)
    shifted = scores - jnp.max(scores, axis=-1, keepdims=True)
    weights = jnp.exp(shifted)
    attn_probs = weights / jnp.sum(weights, axis=-1, keepdims=True)
    return (attn_probs, attn_probs.astype(jnp.bfloat16))


def value_part(probs_low, grad_rows):
    return jnp.einsum("hqk,qhd->kd", probs_low, grad_rows, preferred_element_type=jnp.float32)


def score_part(attn_probs, query_rows, key_cols, value_cols, grad_rows, score_scale):
    dprobs = jnp.einsum("qhd,kd->hqk", grad_rows, value_cols, preferred_element_type=jnp.float32)
    row_dot = jnp.sum(attn_probs * dprobs, axis=-1, keepdims=True)
    dscores = (attn_probs * (dprobs - row_dot)).astype(jnp.bfloat16)
    query_grads = (
        jnp.einsum("hqk,kd->qhd", dscores, key_cols, preferred_element_type=jnp.float32)
        * score_scale
    ).astype(jnp.bfloat16)
    key_grads = (
        jnp.einsum("hqk,qhd->kd", dscores, query_rows, preferred_element_type=jnp.float32)
        * score_scale
    )
    return (query_grads, key_grads)


def fold_heads(received, mp_count):
    block_rows = received.shape[0] // mp_count
    return jnp.sum(received.reshape(KVH, mp_count // KVH, block_rows, received.shape[1]), axis=1)


def head_major(folded):
    return jnp.transpose(folded, (1, 0, 2))


def weight_grad(acts_rows, grads_low, inv_width):
    return (
        lax.dot_general(
            acts_rows, grads_low, (((0,), (0,)), ((), ())), preferred_element_type=jnp.float32
        )
        * inv_width
    )


def sum_values(value_piece, half_kv, mp_count):
    tok_count = value_piece.shape[0]
    block_rows = tok_count // mp_count
    value_received = lax.all_to_all(
        value_piece.astype(jnp.bfloat16), "mp", split_axis=0, concat_axis=0, tiled=True
    ).astype(value_piece.dtype)
    value_block = head_major(fold_heads(value_received, mp_count)).reshape(block_rows, half_kv)
    return lax.all_gather(value_block.astype(jnp.bfloat16), "mp", axis=0, tiled=True)


def sum_keys(key_piece, half_kv, mp_count, cos_block, sin_block):
    tok_count = key_piece.shape[0]
    block_rows = tok_count // mp_count
    key_received = lax.all_to_all(
        key_piece.astype(jnp.bfloat16), "mp", split_axis=0, concat_axis=0, tiled=True
    ).astype(key_piece.dtype)
    key_block = head_major(fold_heads(key_received, mp_count))
    key_plain = unrotate(key_block, cos_block, sin_block).reshape(block_rows, half_kv)
    return lax.all_gather(key_plain.astype(jnp.bfloat16), "mp", axis=0, tiled=True)


def body(acts, queries, keys_values, out_grad, segments, drift, outer_weights, momentum):
    acts_rows = acts[0]
    tok_count = acts_rows.shape[0]
    island_count = lax.axis_size("island")
    mp_count = lax.axis_size("mp")
    block_rows = tok_count // mp_count
    head_dim = HD
    local_heads = queries.shape[2] // head_dim
    kv_width = keys_values.shape[2]
    half_kv = kv_width // 2
    group_size = QH // KVH
    score_scale = 1.0 / math.sqrt(head_dim)
    inv_width = 1.0 / math.sqrt(D)
    kv_index = lax.axis_index("mp") * local_heads // group_size
    block_start = lax.axis_index("mp") * block_rows
    gathered = lax.all_gather(keys_values, "mp", axis=1, tiled=True)[0]
    key_cols = lax.dynamic_slice_in_dim(gathered, kv_index * head_dim, head_dim, 1)
    value_cols = lax.dynamic_slice_in_dim(gathered, half_kv + kv_index * head_dim, head_dim, 1)
    query_rows = queries[0].reshape(tok_count, local_heads, head_dim)
    grad_rows = out_grad[0].reshape(tok_count, local_heads, head_dim)
    segment_ids = segments[0]
    cosine, sine_table = rope_tables(tok_count, head_dim)
    cos_block = lax.dynamic_slice_in_dim(cosine, block_start, block_rows, 0)
    sin_block = lax.dynamic_slice_in_dim(sine_table, block_start, block_rows, 0)
    drift_rows = drift[0]
    attn_probs, probs_low = attention_probs(query_rows, key_cols, segment_ids, score_scale)
    value_piece = value_part(probs_low, grad_rows)
    value_low = sum_values(value_piece, half_kv, mp_count)
    query_grads, key_piece = score_part(
        attn_probs, query_rows, key_cols, value_cols, grad_rows, score_scale
    )
    key_low = sum_keys(key_piece, half_kv, mp_count, cos_block, sin_block)
    grads_low = jnp.concatenate([key_low, value_low], axis=1)
    island_terms = drift_rows.astype(jnp.float32) - INNER_LR * weight_grad(
        acts_rows, grads_low, inv_width
    )
    reduced = lax.psum_scatter(
        island_terms.astype(jnp.bfloat16), "island", scatter_dimension=0, tiled=True
    ).astype(jnp.float32)
    outer_grad = -(reduced / island_count)
    new_momentum = MOMENTUM * momentum[0] + outer_grad
    new_outer = outer_weights[0] - OUTER_LR * (outer_grad + MOMENTUM * new_momentum)
    next_weights = lax.all_gather(new_outer.astype(jnp.bfloat16), "island", axis=0, tiled=True)
    query_out = query_grads.reshape(tok_count, local_heads * head_dim)
    return (query_out[None], new_outer[None], new_momentum[None], next_weights[None])


def solution(mesh):
    in_specs = (
        P("island", None, "mp"),
        P("island", None, "mp"),
        P("island", "mp", None),
        P("island", None, "mp"),
        P("island", None),
        P("island", "mp", None),
        P("mp", "island", None),
        P("mp", "island", None),
    )
    out_specs = (
        P("island", None, "mp"),
        P("mp", "island", None),
        P("mp", "island", None),
        P("mp", None, None),
    )
    return jax.shard_map(body, mesh=mesh, in_specs=in_specs, out_specs=out_specs, check_vma=False)
```

profile of v0, /device:TPU:0, one launch (start us, length us, event | category | flops | bytes accessed | tf_op | source)
XLA Modules:
  0.0 354.0 jit_solution(6495769654644063635)
XLA Ops:
  7.9 3.5 %copy.43 = bf16[128,8,8,128]{3,2,1,0:T(8,128)(2,1)} copy(bf16[128,8,8,128]{3,1,2,0:T(8,128)(2,1)} %bitcast.103) | data formatting | bytes 4194304
  11.5 1.9 copy.44
  14.1 20.8 %all-gather.5.cloned.1.call-done = bf16[1,1024,1024]{2,1,0:T(8,128)(2,1)} async-done(((bf16[1,256,1024]{2,1,0:T(8,128)(2,1)}), bf16[1,1024,1024]{2,1,0:T(8,128)(2,1)}) %all-gather.5.cloned.1.call-update) | async-done | bytes 2097168 | tf_op jit(solution)/shard_map/all_gather | solution.py:132
  34.9 19.1 %fusion.73 = (f32[8,1024]{1,0:T(8,128)S(1)}, f32[8,1024,1024]{1,2,0:T(8,128)}) fusion(pred[1024,1024]{0,1:T(8,128)(4,1)S(1)} %fusion.12, bf16[1024,8,128]{2,1,0:T(8,128)(2,1)} %bitcast.107, bf16[1,1024,1024]{2,1,0:T(8,128)(2,1)} %all-gather.5.cloned.1.call-done, s32[]{:T(128)S(6)} %select_n.20), kind=kOutput, calls=%fused_computation.67 | convolution fusion | flops 2181039104 | bytes 36995076 | tf_op jit(solution)/shard_map/sub | solution.py:53
  53.9 21.3 %fusion.1 = (f32[8,1024]{1,0:T(8,128)S(1)}, f32[1024,1024,8]{1,0,2:T(8,128)}) fusion(f32[8,1024,1024]{1,2,0:T(8,128)} %get-tuple-element.20, f32[8,1024]{1,0:T(8,128)S(1)} %get-tuple-element.19, bf16[1024,8,128]{2,1,0:T(8,128)(2,1)S(1)} %bitcast.105, bf16[1,1024,1024]{2,1,0:T(8,128)(2,1)} %all-gather.5.cloned.1.call-done, s32[]{:T(128)S(6)} %select_n.22), kind=kOutput, calls=%fused_computation.3 | convolution fusion | flops 2172641280 | bytes 69533696 | tf_op jit(solution)/shard_map/qhd,kd->hqk/dot_general | solution.py:64
  75.2 27.9 %fusion.3 = bf16[8,1024,1024]{1,2,0:T(8,128)(2,1)} fusion(f32[1024,1024,8]{1,0,2:T(8,128)} %get-tuple-element.22, f32[8,1024]{1,0:T(8,128)S(1)} %get-tuple-element.21, f32[8,1024,1024]{1,2,0:T(8,128)} %get-tuple-element.20, f32[8,1024]{1,0:T(8,128)S(1)} %get-tuple-element.19), kind=kLoop, calls=%fused_computation.5 | loop fusion | flops 33554432 | bytes 83951616 | tf_op jit(solution)/shard_map/convert_element_type | solution.py:66
  103.1 10.8 %fusion.41 = bf16[1024,128]{1,0:T(8,128)(2,1)S(1)} fusion(bf16[8,1024,1024]{1,2,0:T(8,128)(2,1)} %fusion.3, bf16[1024,8,128]{2,1,0:T(8,128)(2,1)} %bitcast.108), kind=kOutput, calls=%fused_computation.36 | convolution fusion | flops 2147745792 | bytes 19136512 | tf_op jit(solution)/shard_map/hqk,qhd->kd/dot_general | solution.py:72
  114.8 3.4 all-to-all-start
  118.8 5.4 %all-to-all-done = bf16[4,256,128]{1,2,0:T(8,128)(2,1)S(1)} async-done(((bf16[4,256,128]{1,2,0:T(8,128)(2,1)}), bf16[4,256,128]{1,2,0:T(8,128)(2,1)S(1)}, u32[]{:S(2)}, u32[]{:S(2)}) %all-to-all-start) | async-done | bytes 262176 | tf_op jit(solution)/shard_map/all_to_all | solution.py:109
  125.1 13.3 %fusion.44 = bf16[1024,128]{1,0:T(8,128)(2,1)S(1)} fusion(bf16[1024,8,128]{2,1,0:T(8,128)(2,1)S(1)} %bitcast.106, f32[8,1024,1024]{1,2,0:T(8,128)} %get-tuple-element.20, f32[8,1024]{1,0:T(8,128)S(1)} %get-tuple-element.19), kind=kOutput, calls=%fused_computation.37 | convolution fusion | flops 2164391936 | bytes 35946496 | tf_op jit(solution)/shard_map/hqk,qhd->kd/dot_general | solution.py:60
  138.6 9.1 %all_to_all.18 = bf16[4,256,128]{1,2,0:T(8,128)(2,1)} all-to-all(bf16[4,256,128]{1,2,0:T(8,128)(2,1)S(1)} %copy.34), channel_id=1, replica_groups=mesh['island'=8,'mp'=4] {'mp'}, dimensions={0} | all-to-all | bytes 524288 | tf_op jit(solution)/shard_map/all_to_all | solution.py:99
  147.8 6.4 %copy.30 = bf16[1,2048,1024]{1,2,0:T(8,128)(2,1)} copy(bf16[1,2048,1024]{2,1,0:T(8,128)(2,1)} %param.13) | data formatting | bytes 8388608 | tf_op args[5]
  154.2 10.5 %all-gather.9.cloned.1.call-done = bf16[1024,512]{0,1:T(8,128)(2,1)} async-done(((bf16[256,512]{0,1:T(8,128)(2,1)}), bf16[1024,512]{0,1:T(8,128)(2,1)}) %all-gather.9.cloned.1.call-update) | async-done | bytes 1048592 | tf_op jit(solution)/shard_map/all_gather | solution.py:103
  164.7 10.6 %fusion.10 = bf16[2048,1024]{0,1:T(8,128)(2,1)} fusion(bf16[1,2048,1024]{1,2,0:T(8,128)(2,1)} %copy.30, bf16[1,1024,2048]{2,1,0:T(8,128)(2,1)} %param.8, bf16[1024,512]{0,1:T(8,128)(2,1)} %all-gather.9.cloned.1.call-done, bf16[1024,512]{0,1:T(8,128)(2,1)} %all-gather.7.cloned.1.call-done), kind=kOutput, calls=%fused_computation.16 | convolution fusion | flops 4307550208 | bytes 14680064 | tf_op jit(solution)/shard_map/dot_general | solution.py:89
  175.3 1.1 copy-done.2
  176.8 1.6 copy.35
  178.4 85.8 %reduce-scatter.2.cloned.1.call-done = bf16[256,1024]{0,1:T(8,128)(2,1)} async-done(((bf16[2048,1024]{0,1:T(8,128)(2,1)}), bf16[256,1024]{0,1:T(8,128)(2,1)}) %reduce-scatter.2.cloned.1.call-update) | async-done | bytes 524304 | tf_op jit(solution)/shard_map/reduce_scatter | solution.py:153
  264.2 2.5 fusion.71
  266.7 8.5 %multiply_convert_fusion = bf16[128,8,1024]{2,0,1:T(8,128)(2,1)S(1)} fusion(bf16[8,1024,1024]{1,2,0:T(8,128)(2,1)} %fusion.3, bf16[1,1024,1024]{2,1,0:T(8,128)(2,1)} %all-gather.5.cloned.1.call-done, s32[]{:T(128)S(6)} %select_n.20), kind=kOutput, calls=%fused_computation.18 | convolution fusion | flops 2149580800 | bytes 19136516 | tf_op jit(solution)/shard_map/hqk,kd->qhd/dot_general | solution.py:68
  275.2 2.6 copy.36
  277.8 2.5 copy.37
  280.3 1.3 copy.38
  281.6 59.5 %all-gather.11.cloned.1.call-done = bf16[2048,1024]{0,1:T(8,128)(2,1)} async-done(((bf16[256,1024]{0,1:T(8,128)(2,1)}), bf16[2048,1024]{0,1:T(8,128)(2,1)}) %all-gather.11.cloned.1.call-update) | async-done | bytes 4194320 | tf_op jit(solution)/shard_map/all_gather | solution.py:159
  341.1 6.4 %copy.39 = bf16[1,2048,1024]{2,1,0:T(8,128)(2,1)} copy(bf16[1,2048,1024]{1,2,0:T(8,128)(2,1)} %bitcast.102) | data formatting | bytes 8388608
  (28 shorter events, 4.2 us)
Async XLA Ops:
  7.2 4.3 %copy-start = (bf16[1,1024,1024]{2,1,0:T(8,128)(2,1)S(1)}, bf16[1,1024,1024]{2,1,0:T(8,128)(2,1)}, u32[]{:S(2)}) copy-start(bf16[1,1024,1024]{2,1,0:T(8,128)(2,1)} %param.11) | copy-start | bytes 6291460
  7.2 27.7 %all-gather.5.cloned.1.call-start = ((), (), s32[]{:S(2)}) async-start(), calls=%async_computation.3 | async-start | bytes 2621440 | tf_op jit(solution)/shard_map/all_gather | solution.py:132
  7.9 5.5 %copy-start.3 = (s32[1,1024]{1,0:T(1,128)S(1)}, s32[1,1024]{1,0:T(1,128)}, u32[]{:S(2)}) copy-start(s32[1,1024]{1,0:T(1,128)} %param.12) | copy-start | bytes 12292
  34.9 19.1 %copy-start.1 = (bf16[128,8,8,128]{3,2,1,0:T(8,128)(2,1)S(1)}, bf16[128,8,8,128]{3,2,1,0:T(8,128)(2,1)}, u32[]{:S(2)}) copy-start(bf16[128,8,8,128]{3,2,1,0:T(8,128)(2,1)} %copy.44) | copy-start | bytes 6291460
  114.8 9.4 %all-to-all-start = ((bf16[4,256,128]{1,2,0:T(8,128)(2,1)}), bf16[4,256,128]{1,2,0:T(8,128)(2,1)S(1)}, u32[]{:S(2)}, u32[]{:S(2)}) async-start(bf16[4,256,128]{1,2,0:T(8,128)(2,1)} %copy.32), calls=%async_computation | async-start | bytes 524288 | tf_op jit(solution)/shard_map/all_to_all | solution.py:109
  118.3 36.0 %all-gather.7.cloned.1.call-start = ((), (), s32[]{:S(2)}) async-start(), calls=%async_computation.4 | async-start | bytes 1310720 | tf_op jit(solution)/shard_map/all_gather | solution.py:114
  125.1 39.6 %all-gather.9.cloned.1.call-start = ((), (), s32[]{:S(2)}) async-start(), calls=%async_computation.5 | async-start | bytes 1310720 | tf_op jit(solution)/shard_map/all_gather | solution.py:103
  147.7 116.4 %reduce-scatter.2.cloned.1.call-start = ((), (), s32[]{:S(2)}) async-start(), calls=%async_computation.6 | async-start | bytes 4718592 | tf_op jit(solution)/shard_map/reduce_scatter | solution.py:153
  175.3 1.2 copy-start.2
  175.3 165.8 %all-gather.11.cloned.1.call-start = ((), (), s32[]{:S(2)}) async-start(), calls=%async_computation.7 | async-start | bytes 4718592 | tf_op jit(solution)/shard_map/all_gather | solution.py:159
Sparse Core Ops, SparseCore 0:
  9.5 25.2 all-gather.4
  125.2 16.8 all-gather.6
  147.8 16.8 all-gather.8
  175.4 88.6 reduce-scatter.1
  266.8 74.2 all-gather.10
where the time goes:
time: 355 us; the launch traced here: 354 us
  waiting for transfers between devices  183 us (52%)
  matrix products  83.6 us (24%)
  other arithmetic  31.9 us (9%)
  local copies, waits for them, and re-layouts  29 us (8%)
  between operations  13.9 us (4%)
  blocking collectives  9.07 us (3%)
  starting transfers between devices  3.79 us (1%)
    reduce_scatter x1, waiting for transfers between devices, body(): lax.psum_scatter(island_terms.astype(jnp.bfloat16), 'island', scatter_dim...  85.8 us
    all_gather x1, waiting for transfers between devices, body(): lax.all_gather(new_outer.astype(jnp.bfloat16), 'island', axis=0, tiled=True)  59.5 us
    convert_element_type x1, other arithmetic, score_part(): dscores = (attn_probs * (dprobs - row_dot)).astype(jnp.bfloat16)  27.9 us
    unnamed x17, local copies, waits for them, and re-layouts  27.8 us
    dot_general x1, matrix products, score_part(): jnp.einsum('qhd,kd->hqk', grad_rows, value_cols, preferred_element_type=j...  21.3 us
    all_gather x1, waiting for transfers between devices, body(): gathered = lax.all_gather(keys_values, 'mp', axis=1, tiled=True)[0]  20.8 us
    sub x1, matrix products, attention_probs(): shifted = scores - jnp.max(scores, axis=-1, keepdims=True)  19.1 us
    dot_general x1, matrix products, value_part(): jnp.einsum('hqk,qhd->kd', probs_low, grad_rows, preferred_element_type=jn...  13.3 us
  transfers between devices with their start and end apart: 6, of which 5 were waited for; matrix products, arithmetic and copies ran while one was open for 12% of the time, Pallas kernels for 0%

commit v1 on v0

v1 whole, which is shorter than its diff:
```python
import functools
import math

import jax
import jax.numpy as jnp
from jax import lax
from jax.experimental import pallas as pl
from jax.experimental.pallas import tpu as pltpu
from jax.sharding import PartitionSpec as P

D = 8192
HD = 128
QH = 32
KVH = 4

INNER_LR = 0.8
OUTER_LR = 0.7
MOMENTUM = 0.9
ROPE_BASE = 500000.0

TB = 128
UB = 128
NEG = -1e30
LOG2E = 1.4426950408889634
MIB = 1 << 20


def dot_nt(a, b):
    return lax.dot_general(a, b, (((1,), (1,)), ((), ())), preferred_element_type=jnp.float32)


def dot_nn(a, b):
    return lax.dot_general(a, b, (((1,), (0,)), ((), ())), preferred_element_type=jnp.float32)


def rope_tables(positions, head_width):
    half_width = head_width // 2
    exponent = jnp.arange(half_width, dtype=jnp.float32) * (2.0 / head_width)
    frequency = jnp.power(jnp.float32(ROPE_BASE), -exponent)
    angles = jnp.arange(positions, dtype=jnp.float32)[:, None] * frequency[None, :]
    return (jnp.cos(angles), jnp.sin(angles))


def stack_heads(block, heads):
    return jnp.concatenate([block[:, h * HD : (h + 1) * HD] for h in range(heads)], axis=0)


def block_mask(start_row, t_base, u_base):
    u_at = lax.broadcasted_iota(jnp.int32, (UB, TB), 0) + u_base
    t_at = lax.broadcasted_iota(jnp.int32, (UB, TB), 1) + t_base
    return (u_at <= t_at) & (u_at >= start_row)


def fold_rows(x, op):
    parts = [x[i * 8 : (i + 1) * 8] for i in range(x.shape[0] // 8)]
    while len(parts) > 1:
        parts = [op(parts[i], parts[i + 1]) if i + 1 < len(parts) else parts[i] for i in range(0, len(parts), 2)]
    return parts[0]


def value_kernel(low_ref, start_ref, q_ref, g_ref, k_ref, dv_ref, top_ref, inv_ref, s_scr, acc_scr, qc_scr, gc_scr, *, heads, scale2):
    tb = pl.program_id(0)
    width = heads * TB
    low = low_ref[tb]
    high = (tb * TB + TB - 1) // UB + 1

    @pl.when(tb == 0)
    def _():
        acc_scr[...] = jnp.zeros_like(acc_scr)

    for h in range(heads):
        qc_scr[h * TB : (h + 1) * TB, :] = q_ref[:, h * HD : (h + 1) * HD]
        gc_scr[h * TB : (h + 1) * TB, :] = g_ref[:, h * HD : (h + 1) * HD]
    start_row = start_ref[...]

    def scores(ub, top):
        u_base = pl.multiple_of(ub * UB, UB)
        mask = block_mask(start_row, tb * TB, u_base)
        raw = dot_nt(k_ref[pl.ds(u_base, UB), :], qc_scr[...])
        tops = []
        for h in range(heads):
            s = jnp.where(mask, raw[:, h * TB : (h + 1) * TB] * scale2, NEG)
            s_scr[pl.ds(u_base, UB), h * TB : (h + 1) * TB] = s
            tops.append(fold_rows(s, jnp.maximum))
        return jnp.maximum(top, jnp.concatenate(tops, axis=1))

    top8 = lax.fori_loop(low, high, scores, jnp.full((8, width), NEG, jnp.float32))
    top = jnp.max(top8, axis=0, keepdims=True)
    top_ref[0] = top

    def weights(ub, total):
        u_base = pl.multiple_of(ub * UB, UB)
        p = jnp.exp2(s_scr[pl.ds(u_base, UB), :] - top)
        s_scr[pl.ds(u_base, UB), :] = p
        return total + fold_rows(p, jnp.add)

    total8 = lax.fori_loop(low, high, weights, jnp.zeros((8, width), jnp.float32))
    inv = 1.0 / jnp.sum(total8, axis=0, keepdims=True)
    inv_ref[0] = inv

    def grads(ub, carry):
        u_base = pl.multiple_of(ub * UB, UB)
        p = (s_scr[pl.ds(u_base, UB), :] * inv).astype(jnp.bfloat16)
        acc_scr[pl.ds(u_base, UB), :] += dot_nn(p, gc_scr[...])
        return carry

    lax.fori_loop(low, high, grads, 0)

    @pl.when(tb == pl.num_programs(0) - 1)
    def _():
        dv_ref[...] = acc_scr[...].astype(dv_ref.dtype)


def key_kernel(
    low_ref, start_ref, q_ref, g_ref, k_ref, kt_ref, v_ref, top_ref, inv_ref, cos_ref, sin_ref, dk_ref, dq_ref,
    p_scr, d_scr, acc_scr, qc_scr, gc_scr, dqt_scr, *, heads, scale2, scale
):
    tb = pl.program_id(0)
    width = heads * TB
    low = low_ref[tb]
    high = (tb * TB + TB - 1) // UB + 1

    @pl.when(tb == 0)
    def _():
        acc_scr[...] = jnp.zeros_like(acc_scr)

    for h in range(heads):
        qc_scr[h * TB : (h + 1) * TB, :] = q_ref[:, h * HD : (h + 1) * HD]
        gc_scr[h * TB : (h + 1) * TB, :] = g_ref[:, h * HD : (h + 1) * HD]
    start_row = start_ref[...]
    top = top_ref[0]
    inv = inv_ref[0]

    def first(ub, total):
        u_base = pl.multiple_of(ub * UB, UB)
        mask = block_mask(start_row, tb * TB, u_base)
        raw = dot_nt(k_ref[pl.ds(u_base, UB), :], qc_scr[...])
        dp = dot_nt(v_ref[pl.ds(u_base, UB), :], gc_scr[...])
        sums = []
        for h in range(heads):
            cols = slice(h * TB, (h + 1) * TB)
            s = jnp.where(mask, raw[:, cols] * scale2, NEG)
            p = jnp.exp2(s - top[:, cols]) * inv[:, cols]
            p_scr[pl.ds(u_base, UB), cols] = p
            d_scr[pl.ds(u_base, UB), cols] = dp[:, cols]
            sums.append(fold_rows(p * dp[:, cols], jnp.add))
        return total + jnp.concatenate(sums, axis=1)

    total8 = lax.fori_loop(low, high, first, jnp.zeros((8, width), jnp.float32))
    row_dot = jnp.sum(total8, axis=0, keepdims=True)
    dqt_scr[...] = jnp.zeros_like(dqt_scr)

    def second(ub, carry):
        u_base = pl.multiple_of(ub * UB, UB)
        ds = (p_scr[pl.ds(u_base, UB), :] * (d_scr[pl.ds(u_base, UB), :] - row_dot)).astype(jnp.bfloat16)
        acc_scr[pl.ds(u_base, UB), :] += dot_nn(ds, qc_scr[...])
        dqt_scr[...] += dot_nn(kt_ref[:, pl.ds(u_base, UB)], ds)
        return carry

    lax.fori_loop(low, high, second, 0)
    for h in range(heads):
        dq_ref[:, h * HD : (h + 1) * HD] = (dqt_scr[:, h * TB : (h + 1) * TB].T * scale).astype(dq_ref.dtype)

    @pl.when(tb == pl.num_programs(0) - 1)
    def _():
        dk = acc_scr[...] * scale
        dk_ref[...] = (dk * cos_ref[...] + pltpu.roll(dk, HD // 2, 1) * sin_ref[...]).astype(dk_ref.dtype)


def attention_values(low, start, q, g, k, out_dtype):
    tok, cols = q.shape
    heads = cols // HD
    steps = tok // TB
    scale2 = LOG2E / math.sqrt(HD)
    width = heads * TB
    return pl.pallas_call(
        functools.partial(value_kernel, heads=heads, scale2=scale2),
        grid_spec=pltpu.PrefetchScalarGridSpec(
            num_scalar_prefetch=1,
            grid=(steps,),
            in_specs=[
                pl.BlockSpec((1, TB), lambda i, lo: (0, i)),
                pl.BlockSpec((TB, cols), lambda i, lo: (i, 0)),
                pl.BlockSpec((TB, cols), lambda i, lo: (i, 0)),
                pl.BlockSpec((tok, HD), lambda i, lo: (0, 0)),
            ],
            out_specs=[
                pl.BlockSpec((tok, HD), lambda i, lo: (0, 0)),
                pl.BlockSpec((1, 1, width), lambda i, lo: (i, 0, 0)),
                pl.BlockSpec((1, 1, width), lambda i, lo: (i, 0, 0)),
            ],
            scratch_shapes=[
                pltpu.VMEM((tok, width), jnp.float32),
                pltpu.VMEM((tok, HD), jnp.float32),
                pltpu.VMEM((width, HD), jnp.bfloat16),
                pltpu.VMEM((width, HD), jnp.bfloat16),
            ],
        ),
        out_shape=[
            jax.ShapeDtypeStruct((tok, HD), out_dtype),
            jax.ShapeDtypeStruct((steps, 1, width), jnp.float32),
            jax.ShapeDtypeStruct((steps, 1, width), jnp.float32),
        ],
        cost_estimate=pl.CostEstimate(flops=4 * 18 * UB * width * HD, bytes_accessed=2 * tok * cols * 2, transcendentals=0),
        compiler_params=pltpu.CompilerParams(dimension_semantics=("arbitrary",), vmem_limit_bytes=40 * MIB),
        name="value_grads",
    )(low, start, q, g, k)


def attention_keys(low, start, q, g, k, v, top, inv, cos_wide, sin_wide, out_dtype):
    tok, cols = q.shape
    heads = cols // HD
    steps = tok // TB
    width = heads * TB
    return pl.pallas_call(
        functools.partial(key_kernel, heads=heads, scale2=LOG2E / math.sqrt(HD), scale=1.0 / math.sqrt(HD)),
        grid_spec=pltpu.PrefetchScalarGridSpec(
            num_scalar_prefetch=1,
            grid=(steps,),
            in_specs=[
                pl.BlockSpec((1, TB), lambda i, lo: (0, i)),
                pl.BlockSpec((TB, cols), lambda i, lo: (i, 0)),
                pl.BlockSpec((TB, cols), lambda i, lo: (i, 0)),
                pl.BlockSpec((tok, HD), lambda i, lo: (0, 0)),
                pl.BlockSpec((HD, tok), lambda i, lo: (0, 0)),
                pl.BlockSpec((tok, HD), lambda i, lo: (0, 0)),
                pl.BlockSpec((1, 1, width), lambda i, lo: (i, 0, 0)),
                pl.BlockSpec((1, 1, width), lambda i, lo: (i, 0, 0)),
                pl.BlockSpec((tok, HD), lambda i, lo: (0, 0)),
                pl.BlockSpec((tok, HD), lambda i, lo: (0, 0)),
            ],
            out_specs=[
                pl.BlockSpec((tok, HD), lambda i, lo: (0, 0)),
                pl.BlockSpec((TB, cols), lambda i, lo: (i, 0)),
            ],
            scratch_shapes=[
                pltpu.VMEM((tok, width), jnp.float32),
                pltpu.VMEM((tok, width), jnp.float32),
                pltpu.VMEM((tok, HD), jnp.float32),
                pltpu.VMEM((width, HD), jnp.bfloat16),
                pltpu.VMEM((width, HD), jnp.bfloat16),
                pltpu.VMEM((HD, width), jnp.float32),
            ],
        ),
        out_shape=[
            jax.ShapeDtypeStruct((tok, HD), out_dtype),
            jax.ShapeDtypeStruct((tok, cols), jnp.bfloat16),
        ],
        cost_estimate=pl.CostEstimate(flops=8 * 18 * UB * width * HD, bytes_accessed=3 * tok * cols * 2, transcendentals=0),
        compiler_params=pltpu.CompilerParams(dimension_semantics=("arbitrary",), vmem_limit_bytes=40 * MIB),
        name="key_grads",
    )(low, start, q, g, k, k.T, v, top, inv, cos_wide, sin_wide)


def partial_kernel(order_ref, a_ref, g_ref, drift_ref, out_ref, *, factor):
    grad = dot_nn(a_ref[...], g_ref[...])
    out_ref[0] = (drift_ref[...].astype(jnp.float32) - factor * grad).astype(out_ref.dtype)


def island_partials(orders, acts_t, grads, drift, column, factor):
    rows, tok = acts_t.shape
    width = grads.shape[1]
    count = orders.shape[0] // 2
    block = rows // count
    part = width // 2
    out_cols = drift.shape[1] // part
    base = column // part
    return pl.pallas_call(
        functools.partial(partial_kernel, factor=factor),
        grid_spec=pltpu.PrefetchScalarGridSpec(
            num_scalar_prefetch=1,
            grid=(count, 2),
            in_specs=[
                pl.BlockSpec((block, tok), lambda s, d, o: (o[2 * s + d], 0)),
                pl.BlockSpec((tok, part), lambda s, d, o: (0, d)),
                pl.BlockSpec((block, part), lambda s, d, o: (o[2 * s + d], base + d)),
            ],
            out_specs=pl.BlockSpec((1, block, part), lambda s, d, o: (2 * s + d, 0, 0)),
        ),
        out_shape=jax.ShapeDtypeStruct((2 * count, block, part), jnp.bfloat16),
        cost_estimate=pl.CostEstimate(
            flops=2 * rows * tok * width, bytes_accessed=2 * (rows * tok + tok * width + 2 * rows * width), transcendentals=0
        ),
        compiler_params=pltpu.CompilerParams(dimension_semantics=("arbitrary", "arbitrary"), vmem_limit_bytes=32 * MIB),
        name="partials",
    )(orders, acts_t, grads, drift)


def ring_order(count):
    return [i for i in range(0, count, 2)] + [i for i in reversed(range(1, count, 2))]


def ring_tables(count):
    ring = ring_order(count)
    place = [ring.index(i) for i in range(count)]
    up, down = [], []
    for i in range(count):
        up.append([ring[(place[i] - 1 - s) % count] for s in range(count)])
        down.append([ring[(place[i] + 1 + s) % count] for s in range(count)])
    ups = [(ring[i], ring[(i + 1) % count]) for i in range(count)]
    downs = [(ring[i], ring[(i - 1) % count]) for i in range(count)]
    return up, down, ups, downs


def ring_sum(parts, count, direction, perm):
    held = parts[direction]
    for step in range(1, count):
        held = lax.ppermute(held, "island", perm)
        own = parts[2 * step + direction]
        held = held.astype(jnp.float32) + own.astype(jnp.float32)
        if step < count - 1:
            held = held.astype(jnp.bfloat16)
    return held


def fetch_heads(keys_values, mp_count, local_heads):
    half = keys_values.shape[1] // 2
    rows = keys_values.shape[0]
    group = QH // KVH
    me = lax.axis_index("mp")

    def pick(device):
        head = device * local_heads // group
        return jnp.concatenate(
            [
                lax.dynamic_slice_in_dim(keys_values, head * HD, HD, 1),
                lax.dynamic_slice_in_dim(keys_values, half + head * HD, HD, 1),
            ],
            axis=1,
        )

    if mp_count & (mp_count - 1) or mp_count > 4:
        stacked = jnp.stack([pick(j) for j in range(mp_count)])
        return lax.all_to_all(stacked, "mp", split_axis=0, concat_axis=0, tiled=True).reshape(mp_count * rows, 2 * HD)
    whole = jnp.zeros((mp_count, rows, 2 * HD), keys_values.dtype)
    got = [pick(me)] + [
        lax.ppermute(pick(me ^ k), "mp", [(i, i ^ k) for i in range(mp_count)]) for k in range(1, mp_count)
    ]
    for k in range(mp_count):
        whole = lax.dynamic_update_index_in_dim(whole, got[k], me ^ k, 0)
    return whole.reshape(mp_count * rows, 2 * HD)


def gather_columns(piece, mp_count):
    if mp_count != 4:
        return lax.all_gather(piece, "mp", axis=1, tiled=True)
    me = lax.axis_index("mp")
    far = lax.ppermute(piece, "mp", [(i, i ^ 2) for i in range(mp_count)])
    near = lax.ppermute(piece, "mp", [(i, i ^ 1) for i in range(mp_count)])
    far_near = lax.ppermute(far, "mp", [(i, i ^ 1) for i in range(mp_count)])
    odd = (me & 1) == 1
    upper = (me & 2) == 2
    mine = jnp.where(odd, jnp.concatenate([near, piece], 1), jnp.concatenate([piece, near], 1))
    other = jnp.where(odd, jnp.concatenate([far_near, far], 1), jnp.concatenate([far, far_near], 1))
    return jnp.where(upper, jnp.concatenate([other, mine], 1), jnp.concatenate([mine, other], 1))


def fold_and_gather(piece, mp_count):
    tok = piece.shape[0]
    rows = tok // mp_count
    received = lax.all_to_all(piece.astype(jnp.bfloat16), "mp", split_axis=0, concat_axis=0, tiled=True)
    received = received.astype(jnp.float32).reshape(KVH, mp_count // KVH, rows, HD)
    block = jnp.transpose(jnp.sum(received, axis=1), (1, 0, 2)).reshape(rows, KVH * HD)
    return lax.all_gather(block.astype(jnp.bfloat16), "mp", axis=0, tiled=True)


def body(acts, queries, keys_values, out_grad, segments, drift, outer_weights, momentum):
    tok = acts.shape[1]
    island_count = lax.axis_size("island")
    mp_count = lax.axis_size("mp")
    local_heads = queries.shape[2] // HD
    whole_groups = mp_count == KVH
    pair = fetch_heads(keys_values[0], mp_count, local_heads)
    keys, values = pair[:, :HD], pair[:, HD:]
    ids = segments[0]
    start = jnp.sum((ids[None, :] < ids[:, None]).astype(jnp.int32), axis=1)
    low = start[::TB] // UB
    start = start[None, :]
    cosine, sine = rope_tables(tok, HD)
    cos_wide = jnp.concatenate([cosine, cosine], axis=1)
    sin_wide = jnp.concatenate([sine, -sine], axis=1)
    acts_t = acts[0].T
    up, down, ups, downs = ring_tables(island_count)
    me = lax.axis_index("island")
    orders = jnp.stack([jnp.array(up, jnp.int32)[me], jnp.array(down, jnp.int32)[me]], axis=1).reshape(-1)
    factor = INNER_LR / math.sqrt(D)

    piece_type = jnp.bfloat16 if whole_groups else jnp.float32
    q, g = queries[0], out_grad[0]
    value_piece, top, inv = attention_values(low, start, q, g, keys, piece_type)
    gather = gather_columns if whole_groups else fold_and_gather
    value_low = gather(value_piece, mp_count)
    key_piece, query_grads = attention_keys(low, start, q, g, keys, values, top, inv, cos_wide, sin_wide, piece_type)
    half = keys_values.shape[2] // 2
    value_parts = island_partials(orders, acts_t, value_low, drift[0], half, factor)
    key_low = gather(key_piece, mp_count)
    key_parts = island_partials(orders, acts_t, key_low, drift[0], 0, factor)
    columns = []
    for parts in (value_parts, key_parts):
        columns.append([ring_sum(parts, island_count, d, (ups, downs)[d]) for d in range(2)])
    order = [columns[1][0], columns[1][1], columns[0][0], columns[0][1]]
    part = half // 2
    outer, moment, blocks = [], [], []
    for i, total in enumerate(order):
        cols = slice(i * part, (i + 1) * part)
        outer_grad = -(total / island_count)
        new_momentum = MOMENTUM * momentum[0, :, cols] + outer_grad
        new_outer = outer_weights[0, :, cols] - OUTER_LR * (outer_grad + MOMENTUM * new_momentum)
        outer.append(new_outer)
        moment.append(new_momentum)
        blocks.append(new_outer.astype(jnp.bfloat16))
    rows = blocks[0].shape[0]
    gathered = jnp.zeros((island_count, rows, 2 * half), jnp.bfloat16)
    for i in (2, 3, 0, 1):
        held = blocks[i]
        table = (up, down)[i % 2]
        perm = (ups, downs)[i % 2]
        gathered = lax.dynamic_update_slice(gathered, held[None], (me, 0, i * part))
        for step in range(island_count - 1):
            held = lax.ppermute(held, "island", perm)
            owner = orders[2 * step + i % 2]
            gathered = lax.dynamic_update_slice(gathered, held[None], (owner, 0, i * part))
    new_outer = jnp.concatenate(outer, axis=1)
    new_momentum = jnp.concatenate(moment, axis=1)
    next_weights = gathered.reshape(island_count * rows, 2 * half)
    return (query_grads[None], new_outer[None], new_momentum[None], next_weights[None])


def solution(mesh):
    in_specs = (
        P("island", None, "mp"),
        P("island", None, "mp"),
        P("island", "mp", None),
        P("island", None, "mp"),
        P("island", None),
        P("island", "mp", None),
        P("mp", "island", None),
        P("mp", "island", None),
    )
    out_specs = (
        P("island", None, "mp"),
        P("mp", "island", None),
        P("mp", "island", None),
        P("mp", None, None),
    )
    return jax.shard_map(body, mesh=mesh, in_specs=in_specs, out_specs=out_specs, check_vma=False)
```

time: 355 us -> 297 us (0.84)
  matrix products: 83.6 us -> 0 us
  Pallas kernels: 0 us -> 44 us
  starting transfers between devices: 3.79 us -> 41.3 us
  waiting for transfers between devices: 183 us -> 153 us
  other arithmetic: 31.9 us -> 8.42 us
  between operations: 13.9 us -> 27.8 us
  blocking collectives: 9.07 us -> 0 us
  local copies, waits for them, and re-layouts: 29 us -> 22.2 us
    ppermute x0 -> x65, waiting for transfers between devices: none -> 153 us  [the longest x28 129 us: body(): held = lax.ppermute(held, 'island', perm)]
    all_gather x4 -> x0, waiting for transfers between devices: 90.8 us -> none  [the longest x1 59.5 us: body(): lax.all_gather(new_outer.astype(jnp.bfloat16), 'island', axis=0, tiled=True)]
    reduce_scatter x1 -> x0, waiting for transfers between devices: 85.8 us -> none  [body(): lax.psum_scatter(island_terms.astype(jnp.bfloat16), 'island', scatter_dim...]
    dot_general x5 -> x0, matrix products: 64.6 us -> none  [the longest x1 21.3 us: score_part(): jnp.einsum('qhd,kd->hqk', grad_rows, value_cols, preferred_element_type=j...]
    pallas_call x0 -> x4, Pallas kernels: none -> 44 us  [the longest x1 17.3 us: attention_keys(): pl.pallas_call(functools.partial(key_kernel, heads=heads, scale2=LOG2E /...]
    ppermute x0 -> x65, starting transfers between devices: none -> 41.3 us  [the longest x28 28.9 us: ring_sum(): held = lax.ppermute(held, 'island', perm)]
    convert_element_type x2 -> x12, other arithmetic: 30.4 us -> 0.81 us  [ring_sum(): held = held.astype(jnp.bfloat16)]
    sub x1 -> x0, matrix products: 19.1 us -> none  [attention_probs(): shifted = scores - jnp.max(scores, axis=-1, keepdims=True)]
  transfers between devices with their start and end apart: 6 -> 65, of which waited for: 5 -> 47; matrix products, arithmetic and copies ran while one was open for 12% -> 6% of each run, Pallas kernels for 0% -> 10%
where the time goes in v1:
time: 297 us; the launch traced here: 296 us
  waiting for transfers between devices  153 us (52%)
  Pallas kernels  44 us (15%)
  starting transfers between devices  41.3 us (14%)
  between operations  27.8 us (9%)
  local copies, waits for them, and re-layouts  22.2 us (7%)
  other arithmetic  8.42 us (3%)
    ppermute x28, waiting for transfers between devices, body(): held = lax.ppermute(held, 'island', perm)  129 us
    ppermute x28, starting transfers between devices, ring_sum(): held = lax.ppermute(held, 'island', perm)  28.9 us
    ppermute x28, waiting for transfers between devices, ring_sum(): held = lax.ppermute(held, 'island', perm)  21.3 us
    unnamed x19, local copies, waits for them, and re-layouts  18.2 us
    pallas_call x1, Pallas kernels, attention_keys(): pl.pallas_call(functools.partial(key_kernel, heads=heads, scale2=LOG2E /...  17.3 us
    pallas_call x2, Pallas kernels, island_partials(): pl.pallas_call(functools.partial(partial_kernel, factor=factor), grid_spe...  13.4 us
    pallas_call x1, Pallas kernels, attention_values(): pl.pallas_call(functools.partial(value_kernel, heads=heads, scale2=scale2...  13.4 us
    ppermute x28, starting transfers between devices, body(): held = lax.ppermute(held, 'island', perm)  6.23 us
  transfers between devices with their start and end apart: 65, of which 47 were waited for; matrix products, arithmetic and copies ran while one was open for 6% of the time, Pallas kernels for 10%

profile of v1, /device:TPU:0, one launch (start us, length us, event | category | flops | bytes accessed | tf_op | source)
XLA Modules:
  0.0 296.4 jit_solution(8511916769582528695)
XLA Ops:
  15.2 13.4 %value_grads.1 = (bf16[1024,128]{1,0:T(8,128)(2,1)S(1)}, f32[8,1,1024]{2,1,0:T(1,128)S(1)}, f32[8,1,1024]{2,1,0:T(1,128)S(1)}) custom-call(s32[8]{0:T(128)S(1)} %and_select_fusion.low_ref, s32[1,1024]{1,0:T(1,128)S(1)} %bitcast.317, bf16[1024,1024]{1,0:T(8,128)(2,1)S(1)} %bitcast.319, bf16[1024,1024]{1,0:T(8,128)(2,1)S(1)} %bitcast.321, ...), custom_call_target="tpu_custom_call" | custom-call | flops 1207959552 | bytes 4194304 | tf_op jit(solution)/shard_map/value_grads/pallas_call | solution.py:176
  33.7 17.3 %key_grads.1 = (bf16[1024,128]{1,0:T(8,128)(2,1)S(1)}, bf16[1024,1024]{1,0:T(8,128)(2,1)}) custom-call(s32[8]{0:T(128)S(1)} %and_select_fusion.low_ref, s32[1,1024]{1,0:T(1,128)S(1)} %bitcast.318, bf16[1024,1024]{1,0:T(8,128)(2,1)S(1)} %bitcast.320, bf16[1024,1024]{1,0:T(8,128)(2,1)S(1)} %bitcast.322, bf16[1024,128]{1,0:T(8,128)(2,1)S(1)} %get-tuple-element.60.k_ref, ...), custom_call_target="tpu_custom_call" | custom-call | flops 2415919104 | bytes 6291456 | tf_op jit(solution)/shard_map/key_grads/pallas_call | solution.py:215
  71.1 6.4 %copy.22 = bf16[1,1024,2048]{1,2,0:T(8,128)(2,1)} copy(bf16[1,1024,2048]{2,1,0:T(8,128)(2,1)} %param.10) | data formatting | bytes 8388608 | tf_op args[0]
  90.8 6.7 %partials.3 = bf16[16,256,256]{2,1,0:T(8,128)(2,1)S(1)} custom-call(s32[16]{0:T(128)S(1)} %reshape.94.order_ref, bf16[2048,1024]{1,0:T(8,128)(2,1)S(1)} %bitcast.313, bf16[1024,512]{1,0:T(8,128)(2,1)S(1)} %maximum_select_fusion.1.g_ref, bf16[2048,1024]{1,0:T(8,128)(2,1)S(1)} %bitcast.315), custom_call_target="tpu_custom_call" | custom-call | flops 2147483648 | bytes 9437184 | tf_op jit(solution)/shard_map/partials/pallas_call | solution.py:268
  106.3 6.7 %partials.2 = bf16[16,256,256]{2,1,0:T(8,128)(2,1)S(1)} custom-call(s32[16]{0:T(128)S(1)} %reshape.94.order_ref, bf16[2048,1024]{1,0:T(8,128)(2,1)S(1)} %bitcast.314, bf16[1024,512]{1,0:T(8,128)(2,1)S(1)} %maximum_select_fusion.g_ref, bf16[2048,1024]{1,0:T(8,128)(2,1)S(1)} %bitcast.316), custom_call_target="tpu_custom_call" | custom-call | flops 2147483648 | bytes 9437184 | tf_op jit(solution)/shard_map/partials/pallas_call | solution.py:268
  155.7 5.5 %collective-permute-done.38 = bf16[256,256]{1,0:T(8,128)(2,1)S(1)} collective-permute-done((bf16[256,256]{1,0:T(8,128)(2,1)S(1)}, bf16[256,256]{1,0:T(8,128)(2,1)S(1)}, u32[]{:S(2)}, u32[]{:S(2)}) %collective-permute-start.38) | collective-permute-done | bytes 131104 | tf_op jit(solution)/shard_map/ppermute | solution.py:420
  161.4 4.7 %collective-permute-done.39 = bf16[256,256]{1,0:T(8,128)(2,1)S(1)} collective-permute-done((bf16[256,256]{1,0:T(8,128)(2,1)S(1)}, bf16[256,256]{1,0:T(8,128)(2,1)S(1)}, u32[]{:S(2)}, u32[]{:S(2)}) %collective-permute-start.39) | collective-permute-done | bytes 131104 | tf_op jit(solution)/shard_map/ppermute | solution.py:420
  166.4 5.0 %collective-permute-done.40 = bf16[256,256]{1,0:T(8,128)(2,1)S(1)} collective-permute-done((bf16[256,256]{1,0:T(8,128)(2,1)S(1)}, bf16[256,256]{1,0:T(8,128)(2,1)S(1)}, u32[]{:S(2)}, u32[]{:S(2)}) %collective-permute-start.40) | collective-permute-done | bytes 131104 | tf_op jit(solution)/shard_map/ppermute | solution.py:420
  171.6 5.7 %collective-permute-done.41 = bf16[256,256]{1,0:T(8,128)(2,1)S(1)} collective-permute-done((bf16[256,256]{1,0:T(8,128)(2,1)S(1)}, bf16[256,256]{1,0:T(8,128)(2,1)S(1)}, u32[]{:S(2)}, u32[]{:S(2)}) %collective-permute-start.41) | collective-permute-done | bytes 131104 | tf_op jit(solution)/shard_map/ppermute | solution.py:420
  177.3 4.9 %collective-permute-done.42 = bf16[256,256]{1,0:T(8,128)(2,1)S(1)} collective-permute-done((bf16[256,256]{1,0:T(8,128)(2,1)S(1)}, bf16[256,256]{1,0:T(8,128)(2,1)S(1)}, u32[]{:S(2)}, u32[]{:S(2)}) %collective-permute-start.42) | collective-permute-done | bytes 131104 | tf_op jit(solution)/shard_map/ppermute | solution.py:420
  182.3 4.9 %collective-permute-done.43 = bf16[256,256]{1,0:T(8,128)(2,1)S(1)} collective-permute-done((bf16[256,256]{1,0:T(8,128)(2,1)S(1)}, bf16[256,256]{1,0:T(8,128)(2,1)S(1)}, u32[]{:S(2)}, u32[]{:S(2)}) %collective-permute-start.43) | collective-permute-done | bytes 131104 | tf_op jit(solution)/shard_map/ppermute | solution.py:420
  193.9 4.7 %collective-permute-done.45 = bf16[256,256]{1,0:T(8,128)(2,1)S(1)} collective-permute-done((bf16[256,256]{1,0:T(8,128)(2,1)S(1)}, bf16[256,256]{1,0:T(8,128)(2,1)S(1)}, u32[]{:S(2)}, u32[]{:S(2)}) %collective-permute-start.45) | collective-permute-done | bytes 131104 | tf_op jit(solution)/shard_map/ppermute | solution.py:420
  199.0 4.7 %collective-permute-done.46 = bf16[256,256]{1,0:T(8,128)(2,1)S(1)} collective-permute-done((bf16[256,256]{1,0:T(8,128)(2,1)S(1)}, bf16[256,256]{1,0:T(8,128)(2,1)S(1)}, u32[]{:S(2)}, u32[]{:S(2)}) %collective-permute-start.46) | collective-permute-done | bytes 131104 | tf_op jit(solution)/shard_map/ppermute | solution.py:420
  203.9 4.7 %collective-permute-done.47 = bf16[256,256]{1,0:T(8,128)(2,1)S(1)} collective-permute-done((bf16[256,256]{1,0:T(8,128)(2,1)S(1)}, bf16[256,256]{1,0:T(8,128)(2,1)S(1)}, u32[]{:S(2)}, u32[]{:S(2)}) %collective-permute-start.47) | collective-permute-done | bytes 131104 | tf_op jit(solution)/shard_map/ppermute | solution.py:420
  208.9 4.7 %collective-permute-done.48 = bf16[256,256]{1,0:T(8,128)(2,1)S(1)} collective-permute-done((bf16[256,256]{1,0:T(8,128)(2,1)S(1)}, bf16[256,256]{1,0:T(8,128)(2,1)S(1)}, u32[]{:S(2)}, u32[]{:S(2)}) %collective-permute-start.48) | collective-permute-done | bytes 131104 | tf_op jit(solution)/shard_map/ppermute | solution.py:420
  213.9 4.7 %collective-permute-done.49 = bf16[256,256]{1,0:T(8,128)(2,1)S(1)} collective-permute-done((bf16[256,256]{1,0:T(8,128)(2,1)S(1)}, bf16[256,256]{1,0:T(8,128)(2,1)S(1)}, u32[]{:S(2)}, u32[]{:S(2)}) %collective-permute-start.49) | collective-permute-done | bytes 131104 | tf_op jit(solution)/shard_map/ppermute | solution.py:420
  218.8 4.7 %collective-permute-done.50 = bf16[256,256]{1,0:T(8,128)(2,1)S(1)} collective-permute-done((bf16[256,256]{1,0:T(8,128)(2,1)S(1)}, bf16[256,256]{1,0:T(8,128)(2,1)S(1)}, u32[]{:S(2)}, u32[]{:S(2)}) %collective-permute-start.50) | collective-permute-done | bytes 131104 | tf_op jit(solution)/shard_map/ppermute | solution.py:420
  229.6 4.9 %collective-permute-done.52 = bf16[256,256]{1,0:T(8,128)(2,1)S(1)} collective-permute-done((bf16[256,256]{1,0:T(8,128)(2,1)S(1)}, bf16[256,256]{1,0:T(8,128)(2,1)S(1)}, u32[]{:S(2)}, u32[]{:S(2)}) %collective-permute-start.52) | collective-permute-done | bytes 131104 | tf_op jit(solution)/shard_map/ppermute | solution.py:420
  234.6 4.9 %collective-permute-done.53 = bf16[256,256]{1,0:T(8,128)(2,1)S(1)} collective-permute-done((bf16[256,256]{1,0:T(8,128)(2,1)S(1)}, bf16[256,256]{1,0:T(8,128)(2,1)S(1)}, u32[]{:S(2)}, u32[]{:S(2)}) %collective-permute-start.53) | collective-permute-done | bytes 131104 | tf_op jit(solution)/shard_map/ppermute | solution.py:420
  239.6 4.9 %collective-permute-done.54 = bf16[256,256]{1,0:T(8,128)(2,1)S(1)} collective-permute-done((bf16[256,256]{1,0:T(8,128)(2,1)S(1)}, bf16[256,256]{1,0:T(8,128)(2,1)S(1)}, u32[]{:S(2)}, u32[]{:S(2)}) %collective-permute-start.54) | collective-permute-done | bytes 131104 | tf_op jit(solution)/shard_map/ppermute | solution.py:420
  244.5 4.9 %collective-permute-done.55 = bf16[256,256]{1,0:T(8,128)(2,1)S(1)} collective-permute-done((bf16[256,256]{1,0:T(8,128)(2,1)S(1)}, bf16[256,256]{1,0:T(8,128)(2,1)S(1)}, u32[]{:S(2)}, u32[]{:S(2)}) %collective-permute-start.55) | collective-permute-done | bytes 131104 | tf_op jit(solution)/shard_map/ppermute | solution.py:420
  249.5 4.9 %collective-permute-done.56 = bf16[256,256]{1,0:T(8,128)(2,1)S(1)} collective-permute-done((bf16[256,256]{1,0:T(8,128)(2,1)S(1)}, bf16[256,256]{1,0:T(8,128)(2,1)S(1)}, u32[]{:S(2)}, u32[]{:S(2)}) %collective-permute-start.56) | collective-permute-done | bytes 131104 | tf_op jit(solution)/shard_map/ppermute | solution.py:420
  254.5 4.9 %collective-permute-done.57 = bf16[256,256]{1,0:T(8,128)(2,1)S(1)} collective-permute-done((bf16[256,256]{1,0:T(8,128)(2,1)S(1)}, bf16[256,256]{1,0:T(8,128)(2,1)S(1)}, u32[]{:S(2)}, u32[]{:S(2)}) %collective-permute-start.57) | collective-permute-done | bytes 131104 | tf_op jit(solution)/shard_map/ppermute | solution.py:420
  264.9 4.7 %collective-permute-done.59 = bf16[256,256]{1,0:T(8,128)(2,1)S(1)} collective-permute-done((bf16[256,256]{1,0:T(8,128)(2,1)S(1)}, bf16[256,256]{1,0:T(8,128)(2,1)S(1)}, u32[]{:S(2)}, u32[]{:S(2)}) %collective-permute-start.59) | collective-permute-done | bytes 131104 | tf_op jit(solution)/shard_map/ppermute | solution.py:420
  (206 shorter events, 125.1 us)
Async XLA Ops:
  1.9 7.2 %collective-permute-start = (bf16[256,256]{1,0:T(8,128)(2,1)S(1)}, bf16[256,256]{1,0:T(8,128)(2,1)S(1)}, u32[]{:S(2)}, u32[]{:S(2)}) collective-permute-start(bf16[256,256]{1,0:T(8,128)(2,1)S(1)} %pad_maximum_fusion.2), channel_id=1, source_target_pairs={{0,1},{1,0},{2,3},{3,2},{4,5},{5,4},{6,7},{7,6},{8,9},{9,8},{10,11... | collective-permute-start | bytes 393224 | tf_op jit(solution)/shard_map/ppermute | solution.py:337
  2.5 6.9 %collective-permute-start.1 = (bf16[256,256]{1,0:T(8,128)(2,1)S(1)}, bf16[256,256]{1,0:T(8,128)(2,1)S(1)}, u32[]{:S(2)}, u32[]{:S(2)}) collective-permute-start(bf16[256,256]{1,0:T(8,128)(2,1)S(1)} %pad_maximum_fusion.3), channel_id=1, source_target_pairs={{0,2},{1,3},{2,0},{3,1},{4,6},{5,7},{6,4},{7,5},{8,10},{9,11},{10,... | collective-permute-start | bytes 393224 | tf_op jit(solution)/shard_map/ppermute | solution.py:337
  5.1 6.7 %collective-permute-start.2 = (bf16[256,256]{1,0:T(8,128)(2,1)S(1)}, bf16[256,256]{1,0:T(8,128)(2,1)S(1)}, u32[]{:S(2)}, u32[]{:S(2)}) collective-permute-start(bf16[256,256]{1,0:T(8,128)(2,1)S(1)} %pad_maximum_fusion.4), channel_id=1, source_target_pairs={{0,3},{1,2},{2,1},{3,0},{4,7},{5,6},{6,5},{7,4},{8,11},{9,10},{10,... | collective-permute-start | bytes 393224 | tf_op jit(solution)/shard_map/ppermute | solution.py:337
  28.5 58.0 %collective-permute-start.22 = (bf16[1024,128]{1,0:T(8,128)(2,1)S(1)}, bf16[1024,128]{1,0:T(8,128)(2,1)S(1)}, u32[]{:S(2)}, u32[]{:S(2)}) collective-permute-start(bf16[1024,128]{1,0:T(8,128)(2,1)S(1)} %get-tuple-element.13), channel_id=1, source_target_pairs={{0,1},{1,0},{2,3},{3,2},{4,5},{5,4},{6,7},{7,6},{8,9},{9,8},{10,11... | collective-permute-start | bytes 786440 | tf_op jit(solution)/shard_map/ppermute | solution.py:349
  28.7 23.5 %collective-permute-start.20 = (bf16[1024,128]{1,0:T(8,128)(2,1)S(1)}, bf16[1024,128]{1,0:T(8,128)(2,1)S(1)}, u32[]{:S(2)}, u32[]{:S(2)}) collective-permute-start(bf16[1024,128]{1,0:T(8,128)(2,1)S(1)} %get-tuple-element.13), channel_id=1, source_target_pairs={{0,2},{1,3},{2,0},{3,1},{4,6},{5,7},{6,4},{7,5},{8,10},{9,11},{10,... | collective-permute-start | bytes 786440 | tf_op jit(solution)/shard_map/ppermute | solution.py:348
  50.9 35.4 %collective-permute-start.3 = (bf16[1024,128]{1,0:T(8,128)(2,1)S(1)}, bf16[1024,128]{1,0:T(8,128)(2,1)S(1)}, u32[]{:S(2)}, u32[]{:S(2)}) collective-permute-start(bf16[1024,128]{1,0:T(8,128)(2,1)S(1)} %get-tuple-element.12), channel_id=1, source_target_pairs={{0,2},{1,3},{2,0},{3,1},{4,6},{5,7},{6,4},{7,5},{8,10},{9,11},{10,... | collective-permute-start | bytes 786440 | tf_op jit(solution)/shard_map/ppermute | solution.py:348
  52.0 34.7 %collective-permute-start.5 = (bf16[1024,128]{1,0:T(8,128)(2,1)S(1)}, bf16[1024,128]{1,0:T(8,128)(2,1)S(1)}, u32[]{:S(2)}, u32[]{:S(2)}) collective-permute-start(bf16[1024,128]{1,0:T(8,128)(2,1)S(1)} %get-tuple-element.12), channel_id=1, source_target_pairs={{0,1},{1,0},{2,3},{3,2},{4,5},{5,4},{6,7},{7,6},{8,9},{9,8},{10,11... | collective-permute-start | bytes 786440 | tf_op jit(solution)/shard_map/ppermute | solution.py:349
  52.2 34.7 %collective-permute-start.21 = (bf16[1024,128]{1,0:T(8,128)(2,1)S(1)}, bf16[1024,128]{1,0:T(8,128)(2,1)S(1)}, u32[]{:S(2)}, u32[]{:S(2)}) collective-permute-start(bf16[1024,128]{1,0:T(8,128)(2,1)S(1)} %collective-permute-done.20), channel_id=1, source_target_pairs={{0,1},{1,0},{2,3},{3,2},{4,5},{5,4},{6,7},{7,6},{8,9},{9,8},{10,11... | collective-permute-start | bytes 786440 | tf_op jit(solution)/shard_map/ppermute | solution.py:350
  86.4 13.2 %collective-permute-start.4 = (bf16[1024,128]{1,0:T(8,128)(2,1)S(1)}, bf16[1024,128]{1,0:T(8,128)(2,1)S(1)}, u32[]{:S(2)}, u32[]{:S(2)}) collective-permute-start(bf16[1024,128]{1,0:T(8,128)(2,1)S(1)} %collective-permute-done.3), channel_id=1, source_target_pairs={{0,1},{1,0},{2,3},{3,2},{4,5},{5,4},{6,7},{7,6},{8,9},{9,8},{10,11... | collective-permute-start | bytes 786440 | tf_op jit(solution)/shard_map/ppermute | solution.py:350
  97.6 6.6 %collective-permute-start.23 = (bf16[256,256]{1,0:T(8,128)(2,1)S(1)}, bf16[256,256]{1,0:T(8,128)(2,1)S(1)}, u32[]{:S(2)}, u32[]{:S(2)}) collective-permute-start(bf16[256,256]{1,0:T(8,128)(2,1)S(1)} %get-tuple-element.57), channel_id=1, source_target_pairs={{0,8},{8,16},{16,24},{24,28},{28,20},{20,12},{12,4},{4,0},{1,9},{9... | collective-permute-start | bytes 393224 | tf_op jit(solution)/shard_map/ppermute | solution.py:308
  104.2 8.8 %collective-permute-start.31 = (bf16[256,256]{1,0:T(8,128)(2,1)S(1)}, bf16[256,256]{1,0:T(8,128)(2,1)S(1)}, u32[]{:S(2)}, u32[]{:S(2)}) collective-permute-start(bf16[256,256]{1,0:T(8,128)(2,1)S(1)} %get-tuple-element.54), channel_id=1, source_target_pairs={{0,4},{8,0},{16,8},{24,16},{28,24},{20,28},{12,20},{4,12},{1,5},{9... | collective-permute-start | bytes 393224 | tf_op jit(solution)/shard_map/ppermute | solution.py:308
  106.0 7.0 %collective-permute-start.24 = (bf16[256,256]{1,0:T(8,128)(2,1)S(1)}, bf16[256,256]{1,0:T(8,128)(2,1)S(1)}, u32[]{:S(2)}, u32[]{:S(2)}) collective-permute-start(bf16[256,256]{1,0:T(8,128)(2,1)S(1)} %get-tuple-element.55), channel_id=1, source_target_pairs={{0,8},{8,16},{16,24},{24,28},{28,20},{20,12},{12,4},{4,0},{1,9},{9... | collective-permute-start | bytes 393224 | tf_op jit(solution)/shard_map/ppermute | solution.py:308
  115.2 6.8 %collective-permute-start.13 = (bf16[256,256]{1,0:T(8,128)(2,1)S(1)}, bf16[256,256]{1,0:T(8,128)(2,1)S(1)}, u32[]{:S(2)}, u32[]{:S(2)}) collective-permute-start(bf16[256,256]{1,0:T(8,128)(2,1)S(1)} %get-tuple-element.42), channel_id=1, source_target_pairs={{0,4},{8,0},{16,8},{24,16},{28,24},{20,28},{12,20},{4,12},{1,5},{9... | collective-permute-start | bytes 393224 | tf_op jit(solution)/shard_map/ppermute | solution.py:308
  122.9 6.4 %collective-permute-start.14 = (bf16[256,256]{1,0:T(8,128)(2,1)S(1)}, bf16[256,256]{1,0:T(8,128)(2,1)S(1)}, u32[]{:S(2)}, u32[]{:S(2)}) collective-permute-start(bf16[256,256]{1,0:T(8,128)(2,1)S(1)} %get-tuple-element.40), channel_id=1, source_target_pairs={{0,4},{8,0},{16,8},{24,16},{28,24},{20,28},{12,20},{4,12},{1,5},{9... | collective-permute-start | bytes 393224 | tf_op jit(solution)/shard_map/ppermute | solution.py:308
  131.6 6.3 %collective-permute-start.8 = (bf16[256,256]{1,0:T(8,128)(2,1)S(1)}, bf16[256,256]{1,0:T(8,128)(2,1)S(1)}, u32[]{:S(2)}, u32[]{:S(2)}) collective-permute-start(bf16[256,256]{1,0:T(8,128)(2,1)S(1)} %get-tuple-element.39), channel_id=1, source_target_pairs={{0,8},{8,16},{16,24},{24,28},{28,20},{20,12},{12,4},{4,0},{1,9},{9... | collective-permute-start | bytes 393224 | tf_op jit(solution)/shard_map/ppermute | solution.py:308
  133.3 6.8 %collective-permute-start.35 = (bf16[256,256]{1,0:T(8,128)(2,1)S(1)}, bf16[256,256]{1,0:T(8,128)(2,1)S(1)}, u32[]{:S(2)}, u32[]{:S(2)}) collective-permute-start(bf16[256,256]{1,0:T(8,128)(2,1)S(1)} %get-tuple-element.46), channel_id=1, source_target_pairs={{0,4},{8,0},{16,8},{24,16},{28,24},{20,28},{12,20},{4,12},{1,5},{9... | collective-permute-start | bytes 393224 | tf_op jit(solution)/shard_map/ppermute | solution.py:308
  138.5 6.4 %collective-permute-start.9 = (bf16[256,256]{1,0:T(8,128)(2,1)S(1)}, bf16[256,256]{1,0:T(8,128)(2,1)S(1)}, u32[]{:S(2)}, u32[]{:S(2)}) collective-permute-start(bf16[256,256]{1,0:T(8,128)(2,1)S(1)} %get-tuple-element.37), channel_id=1, source_target_pairs={{0,8},{8,16},{16,24},{24,28},{28,20},{20,12},{12,4},{4,0},{1,9},{9... | collective-permute-start | bytes 393224 | tf_op jit(solution)/shard_map/ppermute | solution.py:308
  142.0 6.4 %collective-permute-start.29 = (bf16[256,256]{1,0:T(8,128)(2,1)S(1)}, bf16[256,256]{1,0:T(8,128)(2,1)S(1)}, u32[]{:S(2)}, u32[]{:S(2)}) collective-permute-start(bf16[256,256]{1,0:T(8,128)(2,1)S(1)} %get-tuple-element.45), channel_id=1, source_target_pairs={{0,8},{8,16},{16,24},{24,28},{28,20},{20,12},{12,4},{4,0},{1,9},{9... | collective-permute-start | bytes 393224 | tf_op jit(solution)/shard_map/ppermute | solution.py:308
  149.1 6.3 %collective-permute-start.37 = (bf16[256,256]{1,0:T(8,128)(2,1)S(1)}, bf16[256,256]{1,0:T(8,128)(2,1)S(1)}, u32[]{:S(2)}, u32[]{:S(2)}) collective-permute-start(bf16[256,256]{1,0:T(8,128)(2,1)S(1)} %get-tuple-element.27), channel_id=1, source_target_pairs={{0,8},{8,16},{16,24},{24,28},{28,20},{20,12},{12,4},{4,0},{1,9},{9... | collective-permute-start | bytes 393224 | tf_op jit(solution)/shard_map/ppermute | solution.py:420
  151.2 37.1 %collective-permute-start.18 = (bf16[256,256]{1,0:T(8,128)(2,1)S(1)}, bf16[256,256]{1,0:T(8,128)(2,1)S(1)}, u32[]{:S(2)}, u32[]{:S(2)}) collective-permute-start(bf16[256,256]{1,0:T(8,128)(2,1)S(1)} %get-tuple-element.32), channel_id=1, source_target_pairs={{0,4},{8,0},{16,8},{24,16},{28,24},{20,28},{12,20},{4,12},{1,5},{9... | collective-permute-start | bytes 393224 | tf_op jit(solution)/shard_map/ppermute | solution.py:308
  151.6 36.7 %collective-permute-start.11 = (bf16[256,256]{1,0:T(8,128)(2,1)S(1)}, bf16[256,256]{1,0:T(8,128)(2,1)S(1)}, u32[]{:S(2)}, u32[]{:S(2)}) collective-permute-start(bf16[256,256]{1,0:T(8,128)(2,1)S(1)} %get-tuple-element.33), channel_id=1, source_target_pairs={{0,8},{8,16},{16,24},{24,28},{28,20},{20,12},{12,4},{4,0},{1,9},{9... | collective-permute-start | bytes 393224 | tf_op jit(solution)/shard_map/ppermute | solution.py:308
  153.3 34.0 %collective-permute-start.36 = (bf16[256,256]{1,0:T(8,128)(2,1)S(1)}, bf16[256,256]{1,0:T(8,128)(2,1)S(1)}, u32[]{:S(2)}, u32[]{:S(2)}) collective-permute-start(bf16[256,256]{1,0:T(8,128)(2,1)S(1)} %get-tuple-element.44), channel_id=1, source_target_pairs={{0,4},{8,0},{16,8},{24,16},{28,24},{20,28},{12,20},{4,12},{1,5},{9... | collective-permute-start | bytes 393224 | tf_op jit(solution)/shard_map/ppermute | solution.py:308
  188.3 35.2 %collective-permute-start.12 = (bf16[256,256]{1,0:T(8,128)(2,1)S(1)}, bf16[256,256]{1,0:T(8,128)(2,1)S(1)}, u32[]{:S(2)}, u32[]{:S(2)}) collective-permute-start(bf16[256,256]{1,0:T(8,128)(2,1)S(1)} %get-tuple-element.31), channel_id=1, source_target_pairs={{0,8},{8,16},{16,24},{24,28},{28,20},{20,12},{12,4},{4,0},{1,9},{9... | collective-permute-start | bytes 393224 | tf_op jit(solution)/shard_map/ppermute | solution.py:308
  223.8 35.6 %collective-permute-start.19 = (bf16[256,256]{1,0:T(8,128)(2,1)S(1)}, bf16[256,256]{1,0:T(8,128)(2,1)S(1)}, u32[]{:S(2)}, u32[]{:S(2)}) collective-permute-start(bf16[256,256]{1,0:T(8,128)(2,1)S(1)} %get-tuple-element.30), channel_id=1, source_target_pairs={{0,4},{8,0},{16,8},{24,16},{28,24},{20,28},{12,20},{4,12},{1,5},{9... | collective-permute-start | bytes 393224 | tf_op jit(solution)/shard_map/ppermute | solution.py:308
  (50 other events, 272.5 us)

commit v2 on v1

--- a/solution.py
+++ b/solution.py
@@ -22,7 +22,7 @@
 UB = 128
 NEG = -1e30
 LOG2E = 1.4426950408889634
-MIB = 1 << 20
+VMEM_LIMIT = 60 << 20
 
 
 def dot_nt(a, b):
@@ -202,7 +202,7 @@
             jax.ShapeDtypeStruct((steps, 1, width), jnp.float32),
         ],
         cost_estimate=pl.CostEstimate(flops=4 * 18 * UB * width * HD, bytes_accessed=2 * tok * cols * 2, transcendentals=0),
-        compiler_params=pltpu.CompilerParams(dimension_semantics=("arbitrary",), vmem_limit_bytes=40 * MIB),
+        compiler_params=pltpu.CompilerParams(dimension_semantics=("arbitrary",), vmem_limit_bytes=VMEM_LIMIT),
         name="value_grads",
     )(low, start, q, g, k)
 
@@ -247,7 +247,7 @@
             jax.ShapeDtypeStruct((tok, cols), jnp.bfloat16),
         ],
         cost_estimate=pl.CostEstimate(flops=8 * 18 * UB * width * HD, bytes_accessed=3 * tok * cols * 2, transcendentals=0),
-        compiler_params=pltpu.CompilerParams(dimension_semantics=("arbitrary",), vmem_limit_bytes=40 * MIB),
+        compiler_params=pltpu.CompilerParams(dimension_semantics=("arbitrary",), vmem_limit_bytes=VMEM_LIMIT),
         name="key_grads",
     )(low, start, q, g, k, k.T, v, top, inv, cos_wide, sin_wide)
 
@@ -257,88 +257,114 @@
     out_ref[0] = (drift_ref[...].astype(jnp.float32) - factor * grad).astype(out_ref.dtype)
 
 
-def island_partials(orders, acts_t, grads, drift, column, factor):
+def island_partials(order, acts_t, grads, drift, column, factor):
     rows, tok = acts_t.shape
     width = grads.shape[1]
-    count = orders.shape[0] // 2
+    count = order.shape[0]
     block = rows // count
-    part = width // 2
-    out_cols = drift.shape[1] // part
-    base = column // part
+    base = column // width
     return pl.pallas_call(
         functools.partial(partial_kernel, factor=factor),
         grid_spec=pltpu.PrefetchScalarGridSpec(
             num_scalar_prefetch=1,
-            grid=(count, 2),
+            grid=(count,),
             in_specs=[
-                pl.BlockSpec((block, tok), lambda s, d, o: (o[2 * s + d], 0)),
-                pl.BlockSpec((tok, part), lambda s, d, o: (0, d)),
-                pl.BlockSpec((block, part), lambda s, d, o: (o[2 * s + d], base + d)),
-            ],
-            out_specs=pl.BlockSpec((1, block, part), lambda s, d, o: (2 * s + d, 0, 0)),
+                pl.BlockSpec((block, tok), lambda s, o: (o[s], 0)),
+                pl.BlockSpec((tok, width), lambda s, o: (0, 0)),
+                pl.BlockSpec((block, width), lambda s, o: (o[s], base)),
+            ],
+            out_specs=pl.BlockSpec((1, block, width), lambda s, o: (s, 0, 0)),
         ),
-        out_shape=jax.ShapeDtypeStruct((2 * count, block, part), jnp.bfloat16),
+        out_shape=jax.ShapeDtypeStruct((count, block, width), jnp.bfloat16),
         cost_estimate=pl.CostEstimate(
             flops=2 * rows * tok * width, bytes_accessed=2 * (rows * tok + tok * width + 2 * rows * width), transcendentals=0
         ),
-        compiler_params=pltpu.CompilerParams(dimension_semantics=("arbitrary", "arbitrary"), vmem_limit_bytes=32 * MIB),
+        compiler_params=pltpu.CompilerParams(dimension_semantics=("arbitrary",), vmem_limit_bytes=VMEM_LIMIT),
         name="partials",
-    )(orders, acts_t, grads, drift)
-
-
-def ring_order(count):
-    return [i for i in range(0, count, 2)] + [i for i in reversed(range(1, count, 2))]
-
-
-def ring_tables(count):
-    ring = ring_order(count)
-    place = [ring.index(i) for i in range(count)]
-    up, down = [], []
-    for i in range(count):
-        up.append([ring[(place[i] - 1 - s) % count] for s in range(count)])
-        down.append([ring[(place[i] + 1 + s) % count] for s in range(count)])
-    ups = [(ring[i], ring[(i + 1) % count]) for i in range(count)]
-    downs = [(ring[i], ring[(i - 1) % count]) for i in range(count)]
-    return up, down, ups, downs
-
-
-def ring_sum(parts, count, direction, perm):
-    held = parts[direction]
-    for step in range(1, count):
-        held = lax.ppermute(held, "island", perm)
-        own = parts[2 * step + direction]
-        held = held.astype(jnp.float32) + own.astype(jnp.float32)
-        if step < count - 1:
-            held = held.astype(jnp.bfloat16)
-    return held
-
-
-def fetch_heads(keys_values, mp_count, local_heads):
-    half = keys_values.shape[1] // 2
-    rows = keys_values.shape[0]
+    )(order, acts_t, grads, drift)
+
+
+class Ring:
+    def __init__(self, count):
+        self.count = count
+        self.half = count // 2
+        self.even = count % 2 == 0
+        ring = list(range(0, count, 2)) + list(reversed(range(1, count, 2)))
+        self.ups = [(ring[i], ring[(i + 1) % count]) for i in range(count)]
+        self.downs = [(ring[i], ring[(i - 1) % count]) for i in range(count)]
+        me = lax.axis_index("island")
+        self.place = jnp.where(me % 2 == 0, me // 2, count - 1 - me // 2)
+
+    def at(self, offset):
+        place = lax.rem(self.place + offset + 2 * self.count, self.count)
+        return jnp.where(place < (self.count + 1) // 2, 2 * place, 2 * (self.count - 1 - place) + 1)
+
+    def offsets(self):
+        far = [self.half] if self.even else []
+        full = range(self.half - 1 if self.even else self.half, 0, -1)
+        return far + [sign * s for s in full for sign in (1, -1)] + [0]
+
+    def sum(self, parts):
+        offsets = self.offsets()
+        width = parts.shape[2]
+        halves = (slice(0, width // 2), slice(width // 2, width))
+        held = [None, None]
+        if self.even:
+            held = [
+                lax.ppermute(parts[0][:, halves[d]], "island", (self.ups, self.downs)[d]) for d in range(2)
+            ]
+        at = 1 if self.even else 0
+        first = True
+        while offsets[at] != 0:
+            for d in range(2):
+                own = parts[at + d]
+                if first and self.even:
+                    mine = own[:, halves[d]].astype(jnp.float32) + held[d].astype(jnp.float32)
+                    pieces = [mine.astype(jnp.bfloat16), own[:, halves[1 - d]]]
+                    own = jnp.concatenate(pieces if d == 0 else pieces[::-1], axis=1)
+                elif not first:
+                    own = (own.astype(jnp.float32) + held[d].astype(jnp.float32)).astype(jnp.bfloat16)
+                held[d] = lax.ppermute(own, "island", (self.ups, self.downs)[d])
+            at += 2
+            first = False
+        own = parts[at].astype(jnp.float32)
+        if first and self.even:
+            return own + jnp.concatenate(held, axis=1).astype(jnp.float32)
+        return own + (held[0].astype(jnp.float32) + held[1].astype(jnp.float32))
+
+    def steps(self, block):
+        held = [block, block]
+        full = self.half - 1 if self.even else self.half
+        for step in range(1, full + 1):
+            held = [lax.ppermute(held[d], "island", (self.ups, self.downs)[d]) for d in range(2)]
+            yield [(-step, 0, held[0]), (step, 0, held[1])]
+        if self.even:
+            width = block.shape[1] // 2
+            last = [
+                lax.ppermute(held[d][:, d * width : (d + 1) * width], "island", (self.ups, self.downs)[d])
+                for d in range(2)
+            ]
+            yield [(-self.half, 0, last[0]), (self.half, width, last[1])]
+
+
+def fetch_head(columns, mp_count, local_heads):
+    rows = columns.shape[0]
     group = QH // KVH
     me = lax.axis_index("mp")
 
     def pick(device):
-        head = device * local_heads // group
-        return jnp.concatenate(
-            [
-                lax.dynamic_slice_in_dim(keys_values, head * HD, HD, 1),
-                lax.dynamic_slice_in_dim(keys_values, half + head * HD, HD, 1),
-            ],
-            axis=1,
-        )
-
-    if mp_count & (mp_count - 1) or mp_count > 4:
+        return lax.dynamic_slice_in_dim(columns, device * local_heads // group * HD, HD, 1)
+
+    if mp_count != 4:
         stacked = jnp.stack([pick(j) for j in range(mp_count)])
-        return lax.all_to_all(stacked, "mp", split_axis=0, concat_axis=0, tiled=True).reshape(mp_count * rows, 2 * HD)
-    whole = jnp.zeros((mp_count, rows, 2 * HD), keys_values.dtype)
+        return lax.all_to_all(stacked, "mp", split_axis=0, concat_axis=0, tiled=True).reshape(mp_count * rows, HD)
+    whole = jnp.zeros((mp_count, rows, HD), columns.dtype)
     got = [pick(me)] + [
         lax.ppermute(pick(me ^ k), "mp", [(i, i ^ k) for i in range(mp_count)]) for k in range(1, mp_count)
     ]
     for k in range(mp_count):
         whole = lax.dynamic_update_index_in_dim(whole, got[k], me ^ k, 0)
-    return whole.reshape(mp_count * rows, 2 * HD)
+    return whole.reshape(mp_count * rows, HD)
 
 
 def gather_columns(piece, mp_count):
@@ -370,8 +396,9 @@
     mp_count = lax.axis_size("mp")
     local_heads = queries.shape[2] // HD
     whole_groups = mp_count == KVH
-    pair = fetch_heads(keys_values[0], mp_count, local_heads)
-    keys, values = pair[:, :HD], pair[:, HD:]
+    half = keys_values.shape[2] // 2
+    keys = fetch_head(keys_values[0, :, :half], mp_count, local_heads)
+    values = fetch_head(keys_values[0, :, half:], mp_count, local_heads)
     ids = segments[0]
     start = jnp.sum((ids[None, :] < ids[:, None]).astype(jnp.int32), axis=1)
     low = start[::TB] // UB
@@ -380,9 +407,8 @@
     cos_wide = jnp.concatenate([cosine, cosine], axis=1)
     sin_wide = jnp.concatenate([sine, -sine], axis=1)
     acts_t = acts[0].T
-    up, down, ups, downs = ring_tables(island_count)
-    me = lax.axis_index("island")
-    orders = jnp.stack([jnp.array(up, jnp.int32)[me], jnp.array(down, jnp.int32)[me]], axis=1).reshape(-1)
+    ring = Ring(island_count)
+    order = ring.at(jnp.array(ring.offsets(), jnp.int32))
     factor = INNER_LR / math.sqrt(D)
 
     piece_type = jnp.bfloat16 if whole_groups else jnp.float32
@@ -391,19 +417,13 @@
     gather = gather_columns if whole_groups else fold_and_gather
     value_low = gather(value_piece, mp_count)
     key_piece, query_grads = attention_keys(low, start, q, g, keys, values, top, inv, cos_wide, sin_wide, piece_type)
-    half = keys_values.shape[2] // 2
-    value_parts = island_partials(orders, acts_t, value_low, drift[0], half, factor)
+    value_parts = island_partials(order, acts_t, value_low, drift[0], half, factor)
     key_low = gather(key_piece, mp_count)
-    key_parts = island_partials(orders, acts_t, key_low, drift[0], 0, factor)
-    columns = []
-    for parts in (value_parts, key_parts):
-        columns.append([ring_sum(parts, island_count, d, (ups, downs)[d]) for d in range(2)])
-    order = [columns[1][0], columns[1][1], columns[0][0], columns[0][1]]
-    part = half // 2
+    key_parts = island_partials(order, acts_t, key_low, drift[0], 0, factor)
     outer, moment, blocks = [], [], []
-    for i, total in enumerate(order):
-        cols = slice(i * part, (i + 1) * part)
-        outer_grad = -(total / island_count)
+    for i, parts in enumerate((key_parts, value_parts)):
+        cols = slice(i * half, (i + 1) * half)
+        outer_grad = -(ring.sum(parts) / island_count)
         new_momentum = MOMENTUM * momentum[0, :, cols] + outer_grad
         new_outer = outer_weights[0, :, cols] - OUTER_LR * (outer_grad + MOMENTUM * new_momentum)
         outer.append(new_outer)
@@ -411,15 +431,12 @@
         blocks.append(new_outer.astype(jnp.bfloat16))
     rows = blocks[0].shape[0]
     gathered = jnp.zeros((island_count, rows, 2 * half), jnp.bfloat16)
-    for i in (2, 3, 0, 1):
-        held = blocks[i]
-        table = (up, down)[i % 2]
-        perm = (ups, downs)[i % 2]
-        gathered = lax.dynamic_update_slice(gathered, held[None], (me, 0, i * part))
-        for step in range(island_count - 1):
-            held = lax.ppermute(held, "island", perm)
-            owner = orders[2 * step + i % 2]
-            gathered = lax.dynamic_update_slice(gathered, held[None], (owner, 0, i * part))
+    for i in (1, 0):
+        gathered = lax.dynamic_update_slice(gathered, blocks[i][None], (ring.at(0), 0, i * half))
+    for value_step, key_step in zip(ring.steps(blocks[1]), ring.steps(blocks[0])):
+        for i, arrivals in ((1, value_step), (0, key_step)):
+            for offset, column, block in arrivals:
+                gathered = lax.dynamic_update_slice(gathered, block[None], (ring.at(offset), 0, i * half + column))
     new_outer = jnp.concatenate(outer, axis=1)
     new_momentum = jnp.concatenate(moment, axis=1)
     next_weights = gathered.reshape(island_count * rows, 2 * half)

time: 297 us -> 192 us (0.65)
  waiting for transfers between devices: 153 us -> 60.1 us
  between operations: 27.8 us -> 1.36 us
  other arithmetic: 8.42 us -> 16.5 us
  Pallas kernels: 44 us -> 51.9 us
  local copies, waits for them, and re-layouts: 22.2 us -> 15 us
  starting transfers between devices: 41.3 us -> 46.2 us
    ppermute x59 -> x38, waiting for transfers between devices: 153 us -> 53.2 us  [the longest x12 24.2 us: sum(): held[d] = lax.ppermute(own, 'island', (self.ups, self.downs)[d])]
    unnamed x19 -> x23, local copies, waits for them, and re-layouts: 18.2 us -> 9.18 us
    ppermute x2, waiting for transfers between devices: 0.01 us -> 6.85 us  [gather_columns(): far = lax.ppermute(piece, 'mp', [(i, i ^ 2) for i in range(mp_count)])]
    pallas_call x2, Pallas kernels: 13.4 us -> 18.1 us  [island_partials(): pl.pallas_call(functools.partial(partial_kernel, factor=factor), grid_spe...]
    ppermute x59 -> x38, starting transfers between devices: 38.5 us -> 43.1 us  [the longest x12 14.6 us: sum(): held[d] = lax.ppermute(own, 'island', (self.ups, self.downs)[d])]
    convert_element_type x12 -> x10, other arithmetic: 0.81 us -> 3.82 us  [the longest x6 3.67 us: sum(): (own.astype(jnp.float32) + held[d].astype(jnp.float32)).astype(jnp.bfloat16)]
  transfers between devices with their start and end apart: 65 -> 44, of which waited for: 47 -> 19; matrix products, arithmetic and copies ran while one was open for 6% -> 14% of each run, Pallas kernels for 10% -> 17%
where the time goes in v2:
time: 192 us; the launch traced here: 191 us
  waiting for transfers between devices  60.1 us (31%)
  Pallas kernels  51.9 us (27%)
  starting transfers between devices  46.2 us (24%)
  other arithmetic  16.5 us (9%)
  local copies, waits for them, and re-layouts  15 us (8%)
    ppermute x12, waiting for transfers between devices, sum(): held[d] = lax.ppermute(own, 'island', (self.ups, self.downs)[d])  24.2 us
    pallas_call x1, Pallas kernels, attention_keys(): pl.pallas_call(functools.partial(key_kernel, heads=heads, scale2=LOG2E /...  18.8 us
    pallas_call x2, Pallas kernels, island_partials(): pl.pallas_call(functools.partial(partial_kernel, factor=factor), grid_spe...  18.1 us
    ppermute x12, waiting for transfers between devices, steps(): lax.ppermute(held[d], 'island', (self.ups, self.downs)[d])  17.5 us
    pallas_call x1, Pallas kernels, attention_values(): pl.pallas_call(functools.partial(value_kernel, heads=heads, scale2=scale2...  14.9 us
    ppermute x12, starting transfers between devices, sum(): held[d] = lax.ppermute(own, 'island', (self.ups, self.downs)[d])  14.6 us
    ppermute x12, starting transfers between devices, steps(): lax.ppermute(held[d], 'island', (self.ups, self.downs)[d])  13.2 us
    unnamed x23, local copies, waits for them, and re-layouts  9.18 us
  transfers between devices with their start and end apart: 44, of which 19 were waited for; matrix products, arithmetic and copies ran while one was open for 14% of the time, Pallas kernels for 17%

profile of v2, /device:TPU:0, one launch (start us, length us, event | category | flops | bytes accessed | tf_op | source)
XLA Modules:
  0.0 190.9 jit_solution(15313535233978386627)
XLA Ops:
  2.5 2.6 %collective-permute-start.4 = (bf16[256,128]{1,0:T(8,128)(2,1)S(1)}, bf16[256,128]{1,0:T(8,128)(2,1)S(1)}, u32[]{:S(2)}, u32[]{:S(2)}) collective-permute-start(bf16[256,128]{1,0:T(8,128)(2,1)S(1)} %get-tuple-element.39), channel_id=1, source_target_pairs={{0,2},{1,3},{2,0},{3,1},{4,6},{5,7},{6,4},{7,5},{8,10},{9,11},{10,... | collective-permute-start | bytes 196616 | tf_op jit(solution)/shard_map/ppermute | solution.py:363
  12.8 4.3 %collective-permute-done.2 = bf16[256,128]{1,0:T(8,128)(2,1)S(1)} collective-permute-done((bf16[256,128]{1,0:T(8,128)(2,1)S(1)}, bf16[256,128]{1,0:T(8,128)(2,1)S(1)}, u32[]{:S(2)}, u32[]{:S(2)}) %collective-permute-start.2) | collective-permute-done | bytes 65568 | tf_op jit(solution)/shard_map/ppermute | solution.py:363
  18.0 14.9 %value_grads.1 = (bf16[1024,128]{1,0:T(8,128)(2,1)}, f32[8,1,1024]{2,1,0:T(1,128)}, f32[8,1,1024]{2,1,0:T(1,128)}) custom-call(s32[8]{0:T(128)} %and_select_fusion.low_ref, s32[1,1024]{1,0:T(1,128)} %bitcast.170, bf16[1024,1024]{1,0:T(8,128)(2,1)} %bitcast.172, bf16[1024,1024]{1,0:T(8,128)(2,1)} %bitcast.174, bf16[1024,128]{1,0:T(8,128)(2,1)} %bitcast.165), custom_call_target="tpu_custom_call" | custom-call | flops 1207959552 | bytes 4194304 | tf_op jit(solution)/shard_map/value_grads/pallas_call | solution.py:176
  33.7 18.8 %key_grads.1 = (bf16[1024,128]{1,0:T(8,128)(2,1)}, bf16[1024,1024]{1,0:T(8,128)(2,1)}) custom-call(s32[8]{0:T(128)} %and_select_fusion.low_ref, s32[1,1024]{1,0:T(1,128)} %bitcast.171, bf16[1024,1024]{1,0:T(8,128)(2,1)} %bitcast.173, bf16[1024,1024]{1,0:T(8,128)(2,1)} %bitcast.175, bf16[1024,128]{1,0:T(8,128)(2,1)} %bitcast.166, ...), custom_call_target="tpu_custom_call" | custom-call | flops 2415919104 | bytes 6291456 | tf_op jit(solution)/shard_map/key_grads/pallas_call | solution.py:215
  55.1 6.8 %collective-permute-done.6 = bf16[1024,128]{1,0:T(8,128)(2,1)S(1)} collective-permute-done((bf16[1024,128]{1,0:T(8,128)(2,1)}, bf16[1024,128]{1,0:T(8,128)(2,1)S(1)}, u32[]{:S(2)}, u32[]{:S(2)}) %collective-permute-start.6) | collective-permute-done | bytes 262176 | tf_op jit(solution)/shard_map/ppermute | solution.py:374
  62.4 6.4 %copy.20 = bf16[1,1024,2048]{1,2,0:T(8,128)(2,1)} copy(bf16[1,1024,2048]{2,1,0:T(8,128)(2,1)} %param.9) | data formatting | bytes 8388608 | tf_op args[0]
  71.2 9.0 %partials.2 = bf16[8,256,512]{2,1,0:T(8,128)(2,1)} custom-call(s32[8]{0:T(128)} %compare_select_fusion.2.order_ref, bf16[2048,1024]{1,0:T(8,128)(2,1)} %bitcast.159, bf16[1024,512]{1,0:T(8,128)(2,1)} %maximum_select_fusion.g_ref, bf16[2048,1024]{1,0:T(8,128)(2,1)} %bitcast.161), custom_call_target="tpu_custom_call" | custom-call | flops 2147483648 | bytes 9437184 | tf_op jit(solution)/shard_map/partials/pallas_call | solution.py:266
  81.5 2.7 %collective-permute-start.13 = (bf16[256,256]{1,0:T(8,128)(2,1)S(1)}, bf16[256,256]{1,0:T(8,128)(2,1)S(1)}, u32[]{:S(2)}, u32[]{:S(2)}) collective-permute-start(bf16[256,256]{1,0:T(8,128)(2,1)S(1)} %get-tuple-element.35), channel_id=1, source_target_pairs={{0,4},{8,0},{16,8},{24,16},{28,24},{20,28},{12,20},{4,12},{1,5},{9... | collective-permute-start | bytes 393224 | tf_op jit(solution)/shard_map/ppermute | solution.py:314
  85.7 9.1 %partials.3 = bf16[8,256,512]{2,1,0:T(8,128)(2,1)} custom-call(s32[8]{0:T(128)} %compare_select_fusion.2.order_ref, bf16[2048,1024]{1,0:T(8,128)(2,1)} %bitcast.160, bf16[1024,512]{1,0:T(8,128)(2,1)} %maximum_select_fusion.1.g_ref, bf16[2048,1024]{1,0:T(8,128)(2,1)} %bitcast.162), custom_call_target="tpu_custom_call" | custom-call | flops 2147483648 | bytes 9437184 | tf_op jit(solution)/shard_map/partials/pallas_call | solution.py:266
  100.0 4.8 %collective-permute-done.20 = bf16[256,256]{1,0:T(8,128)(2,1)S(1)} collective-permute-done((bf16[256,256]{1,0:T(8,128)(2,1)S(1)}, bf16[256,256]{1,0:T(8,128)(2,1)S(1)}, u32[]{:S(2)}, u32[]{:S(2)}) %collective-permute-start.20) | collective-permute-done | bytes 131104 | tf_op jit(solution)/shard_map/ppermute | solution.py:314
  107.2 7.7 %collective-permute-done.21 = bf16[256,512]{1,0:T(8,128)(2,1)S(1)} collective-permute-done((bf16[256,512]{1,0:T(8,128)(2,1)S(1)}, bf16[256,512]{1,0:T(8,128)(2,1)S(1)}, u32[]{:S(2)}, u32[]{:S(2)}) %collective-permute-start.21) | collective-permute-done | bytes 262176 | tf_op jit(solution)/shard_map/ppermute | solution.py:327
  117.2 6.9 %collective-permute-done.22 = bf16[256,512]{1,0:T(8,128)(2,1)S(1)} collective-permute-done((bf16[256,512]{1,0:T(8,128)(2,1)S(1)}, bf16[256,512]{1,0:T(8,128)(2,1)S(1)}, u32[]{:S(2)}, u32[]{:S(2)}) %collective-permute-start.22) | collective-permute-done | bytes 262176 | tf_op jit(solution)/shard_map/ppermute | solution.py:327
  130.6 2.7 %collective-permute-done.26 = bf16[256,512]{1,0:T(8,128)(2,1)S(1)} collective-permute-done((bf16[256,512]{1,0:T(8,128)(2,1)S(1)}, bf16[256,512]{1,0:T(8,128)(2,1)S(1)}, u32[]{:S(2)}, u32[]{:S(2)}) %collective-permute-start.26) | collective-permute-done | bytes 262176 | tf_op jit(solution)/shard_map/ppermute | solution.py:327
  134.1 2.3 %collective-permute-start.27 = (bf16[256,512]{1,0:T(8,128)(2,1)}, bf16[256,512]{1,0:T(8,128)(2,1)}, u32[]{:S(2)}, u32[]{:S(2)}) collective-permute-start(bf16[256,512]{1,0:T(8,128)(2,1)} %fusion.1), channel_id=1, source_target_pairs={{0,4},{8,0},{16,8},{24,16},{28,24},{20,28},{12,20},{4,12},{1,5},{9... | collective-permute-start | bytes 786440 | tf_op jit(solution)/shard_map/ppermute | solution.py:327
  136.4 2.6 %collective-permute-done.15 = bf16[256,512]{1,0:T(8,128)(2,1)} collective-permute-done((bf16[256,512]{1,0:T(8,128)(2,1)}, bf16[256,512]{1,0:T(8,128)(2,1)}, u32[]{:S(2)}, u32[]{:S(2)}) %collective-permute-start.15) | collective-permute-done | bytes 262176 | tf_op jit(solution)/shard_map/ppermute | solution.py:327
  140.1 2.5 %collective-permute-start.16 = (bf16[256,512]{1,0:T(8,128)(2,1)S(1)}, bf16[256,512]{1,0:T(8,128)(2,1)S(1)}, u32[]{:S(2)}, u32[]{:S(2)}) collective-permute-start(bf16[256,512]{1,0:T(8,128)(2,1)S(1)} %fusion.7), channel_id=1, source_target_pairs={{0,4},{8,0},{16,8},{24,16},{28,24},{20,28},{12,20},{4,12},{1,5},{9... | collective-permute-start | bytes 786440 | tf_op jit(solution)/shard_map/ppermute | solution.py:327
  146.6 2.4 %collective-permute-start.29 = (bf16[256,512]{1,0:T(8,128)(2,1)S(1)}, bf16[256,512]{1,0:T(8,128)(2,1)S(1)}, u32[]{:S(2)}, u32[]{:S(2)}) collective-permute-start(bf16[256,512]{1,0:T(8,128)(2,1)S(1)} %get-tuple-element.19), channel_id=1, source_target_pairs={{0,4},{8,0},{16,8},{24,16},{28,24},{20,28},{12,20},{4,12},{1,5},{9... | collective-permute-start | bytes 786440 | tf_op jit(solution)/shard_map/ppermute | solution.py:339
  150.5 2.4 %collective-permute-start.31 = (bf16[256,512]{1,0:T(8,128)(2,1)S(1)}, bf16[256,512]{1,0:T(8,128)(2,1)S(1)}, u32[]{:S(2)}, u32[]{:S(2)}) collective-permute-start(bf16[256,512]{1,0:T(8,128)(2,1)S(1)} %get-tuple-element.15), channel_id=1, source_target_pairs={{0,4},{8,0},{16,8},{24,16},{28,24},{20,28},{12,20},{4,12},{1,5},{9... | collective-permute-start | bytes 786440 | tf_op jit(solution)/shard_map/ppermute | solution.py:339
  158.1 3.5 %collective-permute-done.30 = bf16[256,512]{1,0:T(8,128)(2,1)S(1)} collective-permute-done((bf16[256,512]{1,0:T(8,128)(2,1)S(1)}, bf16[256,512]{1,0:T(8,128)(2,1)S(1)}, u32[]{:S(2)}, u32[]{:S(2)}) %collective-permute-start.30) | collective-permute-done | bytes 262176 | tf_op jit(solution)/shard_map/ppermute | solution.py:339
  163.8 3.4 %collective-permute-done.32 = bf16[256,512]{1,0:T(8,128)(2,1)S(1)} collective-permute-done((bf16[256,512]{1,0:T(8,128)(2,1)S(1)}, bf16[256,512]{1,0:T(8,128)(2,1)S(1)}, u32[]{:S(2)}, u32[]{:S(2)}) %collective-permute-start.32) | collective-permute-done | bytes 262176 | tf_op jit(solution)/shard_map/ppermute | solution.py:339
  169.3 3.5 %collective-permute-done.34 = bf16[256,512]{1,0:T(8,128)(2,1)S(1)} collective-permute-done((bf16[256,512]{1,0:T(8,128)(2,1)S(1)}, bf16[256,512]{1,0:T(8,128)(2,1)S(1)}, u32[]{:S(2)}, u32[]{:S(2)}) %collective-permute-start.34) | collective-permute-done | bytes 262176 | tf_op jit(solution)/shard_map/ppermute | solution.py:339
  175.1 3.4 %collective-permute-done.36 = bf16[256,512]{1,0:T(8,128)(2,1)S(1)} collective-permute-done((bf16[256,512]{1,0:T(8,128)(2,1)S(1)}, bf16[256,512]{1,0:T(8,128)(2,1)S(1)}, u32[]{:S(2)}, u32[]{:S(2)}) %collective-permute-start.36) | collective-permute-done | bytes 262176 | tf_op jit(solution)/shard_map/ppermute | solution.py:339
  180.7 2.3 %collective-permute-done.38 = bf16[256,512]{1,0:T(8,128)(2,1)S(1)} collective-permute-done((bf16[256,512]{1,0:T(8,128)(2,1)S(1)}, bf16[256,512]{1,0:T(8,128)(2,1)S(1)}, u32[]{:S(2)}, u32[]{:S(2)}) %collective-permute-start.38) | collective-permute-done | bytes 262176 | tf_op jit(solution)/shard_map/ppermute | solution.py:339
  183.9 2.4 %collective-permute-start.43 = (bf16[256,256]{1,0:T(8,128)(2,1)S(1)}, bf16[256,256]{1,0:T(8,128)(2,1)S(1)}, u32[]{:S(2)}, u32[]{:S(2)}) collective-permute-start(bf16[256,256]{1,0:T(8,128)(2,1)S(1)} %slice.189), channel_id=1, source_target_pairs={{0,4},{8,0},{16,8},{24,16},{28,24},{20,28},{12,20},{4,12},{1,5},{9... | collective-permute-start | bytes 393224 | tf_op jit(solution)/shard_map/ppermute | solution.py:344
  (163 shorter events, 62.1 us)
Async XLA Ops:
  1.9 10.8 %collective-permute-start.3 = (bf16[256,128]{1,0:T(8,128)(2,1)S(1)}, bf16[256,128]{1,0:T(8,128)(2,1)S(1)}, u32[]{:S(2)}, u32[]{:S(2)}) collective-permute-start(bf16[256,128]{1,0:T(8,128)(2,1)S(1)} %get-tuple-element.40), channel_id=1, source_target_pairs={{0,1},{1,0},{2,3},{3,2},{4,5},{5,4},{6,7},{7,6},{8,9},{9,8},{10,11... | collective-permute-start | bytes 196616 | tf_op jit(solution)/shard_map/ppermute | solution.py:363
  2.5 15.4 %collective-permute-start.4 = (bf16[256,128]{1,0:T(8,128)(2,1)S(1)}, bf16[256,128]{1,0:T(8,128)(2,1)S(1)}, u32[]{:S(2)}, u32[]{:S(2)}) collective-permute-start(bf16[256,128]{1,0:T(8,128)(2,1)S(1)} %get-tuple-element.39), channel_id=1, source_target_pairs={{0,2},{1,3},{2,0},{3,1},{4,6},{5,7},{6,4},{7,5},{8,10},{9,11},{10,... | collective-permute-start | bytes 196616 | tf_op jit(solution)/shard_map/ppermute | solution.py:363
  5.1 27.8 %collective-permute-start.5 = (bf16[256,128]{1,0:T(8,128)(2,1)S(1)}, bf16[256,128]{1,0:T(8,128)(2,1)S(1)}, u32[]{:S(2)}, u32[]{:S(2)}) collective-permute-start(bf16[256,128]{1,0:T(8,128)(2,1)S(1)} %get-tuple-element.38), channel_id=1, source_target_pairs={{0,3},{1,2},{2,1},{3,0},{4,7},{5,6},{6,5},{7,4},{8,11},{9,10},{10,... | collective-permute-start | bytes 196616 | tf_op jit(solution)/shard_map/ppermute | solution.py:363
  52.5 16.3 %collective-permute-start.17 = (bf16[1024,128]{1,0:T(8,128)(2,1)S(1)}, bf16[1024,128]{1,0:T(8,128)(2,1)S(1)}, u32[]{:S(2)}, u32[]{:S(2)}) collective-permute-start(bf16[1024,128]{1,0:T(8,128)(2,1)S(1)} %copy-done.7), channel_id=1, source_target_pairs={{0,2},{1,3},{2,0},{3,1},{4,6},{5,7},{6,4},{7,5},{8,10},{9,11},{10,... | collective-permute-start | bytes 786440 | tf_op jit(solution)/shard_map/ppermute | solution.py:374
  54.5 14.8 %collective-permute-start.8 = (bf16[1024,128]{1,0:T(8,128)(2,1)}, bf16[1024,128]{1,0:T(8,128)(2,1)S(1)}, u32[]{:S(2)}, u32[]{:S(2)}) collective-permute-start(bf16[1024,128]{1,0:T(8,128)(2,1)} %get-tuple-element.12), channel_id=1, source_target_pairs={{0,1},{1,0},{2,3},{3,2},{4,5},{5,4},{6,7},{7,6},{8,9},{9,8},{10,11... | collective-permute-start | bytes 786440 | tf_op jit(solution)/shard_map/ppermute | solution.py:375
  54.5 15.0 %collective-permute-start.19 = (bf16[1024,128]{1,0:T(8,128)(2,1)S(1)}, bf16[1024,128]{1,0:T(8,128)(2,1)S(1)}, u32[]{:S(2)}, u32[]{:S(2)}) collective-permute-start(bf16[1024,128]{1,0:T(8,128)(2,1)S(1)} %copy-done.7), channel_id=1, source_target_pairs={{0,1},{1,0},{2,3},{3,2},{4,5},{5,4},{6,7},{7,6},{8,9},{9,8},{10,11... | collective-permute-start | bytes 786440 | tf_op jit(solution)/shard_map/ppermute | solution.py:375
  68.9 15.4 %collective-permute-start.18 = (bf16[1024,128]{1,0:T(8,128)(2,1)S(1)}, bf16[1024,128]{1,0:T(8,128)(2,1)S(1)}, u32[]{:S(2)}, u32[]{:S(2)}) collective-permute-start(bf16[1024,128]{1,0:T(8,128)(2,1)S(1)} %collective-permute-done.17), channel_id=1, source_target_pairs={{0,1},{1,0},{2,3},{3,2},{4,5},{5,4},{6,7},{7,6},{8,9},{9,8},{10,11... | collective-permute-start | bytes 786440 | tf_op jit(solution)/shard_map/ppermute | solution.py:376
  81.5 25.7 %collective-permute-start.13 = (bf16[256,256]{1,0:T(8,128)(2,1)S(1)}, bf16[256,256]{1,0:T(8,128)(2,1)S(1)}, u32[]{:S(2)}, u32[]{:S(2)}) collective-permute-start(bf16[256,256]{1,0:T(8,128)(2,1)S(1)} %get-tuple-element.35), channel_id=1, source_target_pairs={{0,4},{8,0},{16,8},{24,16},{28,24},{20,28},{12,20},{4,12},{1,5},{9... | collective-permute-start | bytes 393224 | tf_op jit(solution)/shard_map/ppermute | solution.py:314
  84.2 14.1 %collective-permute-start.9 = (bf16[256,256]{1,0:T(8,128)(2,1)S(1)}, bf16[256,256]{1,0:T(8,128)(2,1)S(1)}, u32[]{:S(2)}, u32[]{:S(2)}) collective-permute-start(bf16[256,256]{1,0:T(8,128)(2,1)S(1)} %get-tuple-element.34), channel_id=1, source_target_pairs={{0,8},{8,16},{16,24},{24,28},{28,20},{20,12},{12,4},{4,0},{1,9},{9... | collective-permute-start | bytes 393224 | tf_op jit(solution)/shard_map/ppermute | solution.py:314
  98.3 18.8 %collective-permute-start.10 = (bf16[256,512]{1,0:T(8,128)(2,1)S(1)}, bf16[256,512]{1,0:T(8,128)(2,1)S(1)}, u32[]{:S(2)}, u32[]{:S(2)}) collective-permute-start(bf16[256,512]{1,0:T(8,128)(2,1)S(1)} %pad_maximum_fusion.2), channel_id=1, source_target_pairs={{0,8},{8,16},{16,24},{24,28},{28,20},{20,12},{12,4},{4,0},{1,9},{9... | collective-permute-start | bytes 786440 | tf_op jit(solution)/shard_map/ppermute | solution.py:327
  105.1 12.2 %collective-permute-start.25 = (bf16[256,512]{1,0:T(8,128)(2,1)S(1)}, bf16[256,512]{1,0:T(8,128)(2,1)S(1)}, u32[]{:S(2)}, u32[]{:S(2)}) collective-permute-start(bf16[256,512]{1,0:T(8,128)(2,1)S(1)} %pad_maximum_fusion.5), channel_id=1, source_target_pairs={{0,4},{8,0},{16,8},{24,16},{28,24},{20,28},{12,20},{4,12},{1,5},{9... | collective-permute-start | bytes 786440 | tf_op jit(solution)/shard_map/ppermute | solution.py:327
  115.0 11.7 %collective-permute-start.14 = (bf16[256,512]{1,0:T(8,128)(2,1)S(1)}, bf16[256,512]{1,0:T(8,128)(2,1)S(1)}, u32[]{:S(2)}, u32[]{:S(2)}) collective-permute-start(bf16[256,512]{1,0:T(8,128)(2,1)S(1)} %pad_maximum_fusion.3), channel_id=1, source_target_pairs={{0,4},{8,0},{16,8},{24,16},{28,24},{20,28},{12,20},{4,12},{1,5},{9... | collective-permute-start | bytes 786440 | tf_op jit(solution)/shard_map/ppermute | solution.py:327
  130.1 12.5 %collective-permute-start.23 = (bf16[256,512]{1,0:T(8,128)(2,1)}, bf16[256,512]{1,0:T(8,128)(2,1)S(1)}, u32[]{:S(2)}, u32[]{:S(2)}) collective-permute-start(bf16[256,512]{1,0:T(8,128)(2,1)} %get-tuple-element.27), channel_id=1, source_target_pairs={{0,8},{8,16},{16,24},{24,28},{28,20},{20,12},{12,4},{4,0},{1,9},{9... | collective-permute-start | bytes 786440 | tf_op jit(solution)/shard_map/ppermute | solution.py:327
  134.1 10.6 %collective-permute-start.27 = (bf16[256,512]{1,0:T(8,128)(2,1)}, bf16[256,512]{1,0:T(8,128)(2,1)}, u32[]{:S(2)}, u32[]{:S(2)}) collective-permute-start(bf16[256,512]{1,0:T(8,128)(2,1)} %fusion.1), channel_id=1, source_target_pairs={{0,4},{8,0},{16,8},{24,16},{28,24},{20,28},{12,20},{4,12},{1,5},{9... | collective-permute-start | bytes 786440 | tf_op jit(solution)/shard_map/ppermute | solution.py:327
  136.4 12.5 %collective-permute-start.12 = (bf16[256,512]{1,0:T(8,128)(2,1)}, bf16[256,512]{1,0:T(8,128)(2,1)S(1)}, u32[]{:S(2)}, u32[]{:S(2)}) collective-permute-start(bf16[256,512]{1,0:T(8,128)(2,1)} %get-tuple-element.22), channel_id=1, source_target_pairs={{0,8},{8,16},{16,24},{24,28},{28,20},{20,12},{12,4},{4,0},{1,9},{9... | collective-permute-start | bytes 786440 | tf_op jit(solution)/shard_map/ppermute | solution.py:327
  150.4 11.2 %collective-permute-start.30 = (bf16[256,512]{1,0:T(8,128)(2,1)S(1)}, bf16[256,512]{1,0:T(8,128)(2,1)S(1)}, u32[]{:S(2)}, u32[]{:S(2)}) collective-permute-start(bf16[256,512]{1,0:T(8,128)(2,1)S(1)} %get-tuple-element.15), channel_id=1, source_target_pairs={{0,8},{8,16},{16,24},{24,28},{28,20},{20,12},{12,4},{4,0},{1,9},{9... | collective-permute-start | bytes 786440 | tf_op jit(solution)/shard_map/ppermute | solution.py:339
  150.5 11.1 %collective-permute-start.31 = (bf16[256,512]{1,0:T(8,128)(2,1)S(1)}, bf16[256,512]{1,0:T(8,128)(2,1)S(1)}, u32[]{:S(2)}, u32[]{:S(2)}) collective-permute-start(bf16[256,512]{1,0:T(8,128)(2,1)S(1)} %get-tuple-element.15), channel_id=1, source_target_pairs={{0,4},{8,0},{16,8},{24,16},{28,24},{20,28},{12,20},{4,12},{1,5},{9... | collective-permute-start | bytes 786440 | tf_op jit(solution)/shard_map/ppermute | solution.py:339
  156.0 11.2 %collective-permute-start.32 = (bf16[256,512]{1,0:T(8,128)(2,1)S(1)}, bf16[256,512]{1,0:T(8,128)(2,1)S(1)}, u32[]{:S(2)}, u32[]{:S(2)}) collective-permute-start(bf16[256,512]{1,0:T(8,128)(2,1)S(1)} %collective-permute-done.28), channel_id=1, source_target_pairs={{0,8},{8,16},{16,24},{24,28},{28,20},{20,12},{12,4},{4,0},{1,9},{9... | collective-permute-start | bytes 786440 | tf_op jit(solution)/shard_map/ppermute | solution.py:339
  156.0 11.2 %collective-permute-start.33 = (bf16[256,512]{1,0:T(8,128)(2,1)S(1)}, bf16[256,512]{1,0:T(8,128)(2,1)S(1)}, u32[]{:S(2)}, u32[]{:S(2)}) collective-permute-start(bf16[256,512]{1,0:T(8,128)(2,1)S(1)} %collective-permute-done.29), channel_id=1, source_target_pairs={{0,4},{8,0},{16,8},{24,16},{28,24},{20,28},{12,20},{4,12},{1,5},{9... | collective-permute-start | bytes 786440 | tf_op jit(solution)/shard_map/ppermute | solution.py:339
  161.6 11.2 %collective-permute-start.34 = (bf16[256,512]{1,0:T(8,128)(2,1)S(1)}, bf16[256,512]{1,0:T(8,128)(2,1)S(1)}, u32[]{:S(2)}, u32[]{:S(2)}) collective-permute-start(bf16[256,512]{1,0:T(8,128)(2,1)S(1)} %collective-permute-done.30), channel_id=1, source_target_pairs={{0,8},{8,16},{16,24},{24,28},{28,20},{20,12},{12,4},{4,0},{1,9},{9... | collective-permute-start | bytes 786440 | tf_op jit(solution)/shard_map/ppermute | solution.py:339
  161.6 11.2 %collective-permute-start.35 = (bf16[256,512]{1,0:T(8,128)(2,1)S(1)}, bf16[256,512]{1,0:T(8,128)(2,1)S(1)}, u32[]{:S(2)}, u32[]{:S(2)}) collective-permute-start(bf16[256,512]{1,0:T(8,128)(2,1)S(1)} %collective-permute-done.31), channel_id=1, source_target_pairs={{0,4},{8,0},{16,8},{24,16},{28,24},{20,28},{12,20},{4,12},{1,5},{9... | collective-permute-start | bytes 786440 | tf_op jit(solution)/shard_map/ppermute | solution.py:339
  167.2 11.2 %collective-permute-start.36 = (bf16[256,512]{1,0:T(8,128)(2,1)S(1)}, bf16[256,512]{1,0:T(8,128)(2,1)S(1)}, u32[]{:S(2)}, u32[]{:S(2)}) collective-permute-start(bf16[256,512]{1,0:T(8,128)(2,1)S(1)} %collective-permute-done.32), channel_id=1, source_target_pairs={{0,8},{8,16},{16,24},{24,28},{28,20},{20,12},{12,4},{4,0},{1,9},{9... | collective-permute-start | bytes 786440 | tf_op jit(solution)/shard_map/ppermute | solution.py:339
  167.2 11.3 %collective-permute-start.37 = (bf16[256,512]{1,0:T(8,128)(2,1)S(1)}, bf16[256,512]{1,0:T(8,128)(2,1)S(1)}, u32[]{:S(2)}, u32[]{:S(2)}) collective-permute-start(bf16[256,512]{1,0:T(8,128)(2,1)S(1)} %collective-permute-done.33), channel_id=1, source_target_pairs={{0,4},{8,0},{16,8},{24,16},{28,24},{20,28},{12,20},{4,12},{1,5},{9... | collective-permute-start | bytes 786440 | tf_op jit(solution)/shard_map/ppermute | solution.py:339
  172.9 11.0 %collective-permute-start.39 = (bf16[256,512]{1,0:T(8,128)(2,1)S(1)}, bf16[256,512]{1,0:T(8,128)(2,1)S(1)}, u32[]{:S(2)}, u32[]{:S(2)}) collective-permute-start(bf16[256,512]{1,0:T(8,128)(2,1)S(1)} %collective-permute-done.35), channel_id=1, source_target_pairs={{0,4},{8,0},{16,8},{24,16},{28,24},{20,28},{12,20},{4,12},{1,5},{9... | collective-permute-start | bytes 786440 | tf_op jit(solution)/shard_map/ppermute | solution.py:339
  (31 other events, 303.8 us)
